TPU v7x, 32 devices: a whole 2x2x4 slice. The times are simulated.
32 devices in a mesh: cuts: 2 (over x), region: 16 (over z, y, core).
Axes of the slice: x: 2, y: 2, z: 4, core: 2. Of those that a mesh axis runs over, the one named last changes fastest.
Arguments:
- objects: float32 [2, 2, 4096, 1024], P('cuts', None, 'region'), may hold values from -4 to 4
- probes: bfloat16 [4, 2, 256, 256], replicated, may hold values from -4 to 4
- amplitudes: float32 [64, 256, 256], P('region'), may hold values from 0.2 to 2.5
- prop_phase: float32 [256, 256], replicated, may hold values from -3.140625 to 3.140625
- scan_rows: int32 [64], P('region'), may hold values from -128 to 128, as said below
- scan_cols: int32 [64], P('region'), may hold values from 0 to 768
- probe_choice: int32 [64], P('region'), may hold values from 0 to 3
Outputs:
- gradient: float32 [2, 2, 4096, 1024], P('cuts', None, 'region')
Inputs may be any that keep to these rules, and one draw needn't show every extreme that they name: `scan_rows`: in every region, half of the positions start between 64 and 128 rows above the band's first row, and the other half end between 64 and 128 rows below its last row.
All inputs are finite; a program needn't handle non-finite values.
Results may differ from a plain program's by a relative error of at most 0.039.
Values may be sent and summed in bfloat16 or wider, within the bound.
A program may use at most 64 MiB of HBM per device.

v0:
```python
import jax
import jax.numpy as jnp
from jax import lax
from jax.sharding import PartitionSpec as P

modulus_floor = 0.25


def padded(block, sides, width):
    for axis, dim in sides:
        count = lax.axis_size(axis)
        forward = [(i, i + 1) for i in range(count - 1)]
        forward.append((count - 1, 0))
        backward = [(target, source) for source, target in forward]
        low = lax.ppermute(
            lax.slice_in_dim(block, block.shape[dim] - width, None, axis=dim), axis, forward
        )
        high = lax.ppermute(lax.slice_in_dim(block, 0, width, axis=dim), axis, backward)
        block = jnp.concatenate([low, block, high], axis=dim)
    return block


def from_behind(block, axis, distance):
    devices = range(lax.axis_size(axis))
    route = [(i - distance, i) for i in devices if i - distance in devices]
    return lax.ppermute(block, axis, route)


def widened(narrow):
    return lax.optimization_barrier(narrow).astype(jnp.float32)


def dft_tables(length, direction):
    indices = jnp.arange(length, dtype=jnp.int32)
    product = indices[:, None] * indices[None, :] % length
    angles = product.astype(jnp.float32) * (2.0 * jnp.pi / length)
    scaling = 1.0 / jnp.sqrt(jnp.float32(length))
    table = jnp.stack([jnp.cos(angles) * scaling, direction * jnp.sin(angles) * scaling]).astype(
        jnp.bfloat16
    )
    real_table = table[0]
    imag_table = table[1]
    negated = -imag_table
    left_block = jnp.stack([jnp.stack([real_table, negated]), jnp.stack([imag_table, real_table])])
    right_block = jnp.stack([jnp.stack([real_table, imag_table]), jnp.stack([negated, real_table])])
    return (left_block, right_block)


def transform(input_field, block_tables):
    left_block, right_block = block_tables
    middle = jnp.einsum(
        "dcjk,nckl->ndjl",
        left_block,
        input_field.astype(jnp.bfloat16),
        preferred_element_type=jnp.float32,
    ).astype(jnp.bfloat16)
    return jnp.einsum("nckl,cdlm->ndkm", middle, right_block, preferred_element_type=jnp.float32)


def multiply_complex(left_field, right_field):
    real_part = (
        left_field[..., 0, :, :] * right_field[..., 0, :, :]
        - left_field[..., 1, :, :] * right_field[..., 1, :, :]
    )
    imag_part = (
        left_field[..., 0, :, :] * right_field[..., 1, :, :]
        + left_field[..., 1, :, :] * right_field[..., 0, :, :]
    )
    return jnp.stack([real_part, imag_part], axis=-3)


def multiply_conjugate(left_field, right_field):
    real_part = (
        left_field[..., 0, :, :] * right_field[..., 0, :, :]
        + left_field[..., 1, :, :] * right_field[..., 1, :, :]
    )
    imag_part = (
        left_field[..., 0, :, :] * right_field[..., 1, :, :]
        - left_field[..., 1, :, :] * right_field[..., 0, :, :]
    )
    return jnp.stack([real_part, imag_part], axis=-3)


def propagate_adjoint(input_field, optics):
    propagator, forward_table, inverse_table = optics
    return transform(
        multiply_conjugate(propagator, transform(input_field, forward_table)), inverse_table
    )


def forward_slices(incoming, patch_set, measured, optics, last_cut):
    current = incoming
    stored = [current]
    exit_field = multiply_complex(widened(current), patch_set[:, 0])
    far_field = transform(exit_field, optics[1])
    modulus = jnp.sqrt(far_field[:, 0] * far_field[:, 0] + far_field[:, 1] * far_field[:, 1])
    factor = 1.0 - measured / jnp.maximum(modulus, modulus_floor)
    detected = far_field * factor[:, None]
    onward = multiply_complex(optics[0], far_field)
    chosen = jnp.where(last_cut, detected, onward)
    current = transform(chosen, optics[2]).astype(jnp.bfloat16)
    return (jnp.stack(stored, axis=1), current)


def adjoint_slices(seed_wave, stored_set, patch_set, optics):
    local_count = patch_set.shape[1]
    current = seed_wave
    pieces = [None] * local_count
    for slice_index in reversed(range(local_count)):
        arriving = widened(current)
        pieces[slice_index] = multiply_conjugate(widened(stored_set[:, slice_index]), arriving)
        backward = multiply_conjugate(patch_set[:, slice_index], arriving)
        current = propagate_adjoint(backward, optics).astype(jnp.bfloat16)
    return (jnp.stack(pieces, axis=1), current)


def cut_patches(extended, top_rows, left_cols, rim_depth, patch_side):
    zero_index = jnp.zeros((), jnp.int32)

    def window(top_row, left_col):
        return lax.dynamic_slice(
            extended,
            (zero_index, zero_index, top_row + rim_depth, left_col),
            (extended.shape[0], 2, patch_side, patch_side),
        )

    return jax.vmap(window)(top_rows, left_cols)


def add_patches(gradient, pieces, top_rows, left_cols, rim_depth):
    zero_index = jnp.zeros((), jnp.int32)

    def deposit(position, running):
        corner = (zero_index, zero_index, top_rows[position] + rim_depth, left_cols[position])
        existing = lax.dynamic_slice(running, corner, pieces.shape[1:])
        return lax.dynamic_update_slice(running, existing + pieces[position], corner)

    return lax.fori_loop(0, pieces.shape[0], deposit, gradient)


def select_probes(probes, probe_choice):
    mode_ids = jnp.arange(probes.shape[0], dtype=jnp.int32)
    picked = probe_choice[:, None] == mode_ids[None, :]
    return jnp.sum(
        jnp.where(picked[:, :, None, None, None], probes[None], jnp.zeros((), probes.dtype)), axis=1
    )


def shards(objects, probes, amplitudes, prop_phase, scan_rows, scan_cols, probe_choice):
    patch_side = probes.shape[-1]
    rim_depth = patch_side // 2
    band_rows = objects.shape[2]
    optics = (
        jnp.stack([jnp.cos(prop_phase), jnp.sin(prop_phase)]),
        dft_tables(patch_side, -1.0),
        dft_tables(patch_side, 1.0),
    )
    cut_index = lax.axis_index("cuts")
    cut_count = lax.axis_size("cuts")
    first_cut = cut_index == 0
    last_cut = cut_index == cut_count - 1
    extended = padded(objects, (("region", 2),), rim_depth)
    patches = cut_patches(extended, scan_rows, scan_cols, rim_depth, patch_side)
    illumination = select_probes(probes, probe_choice)

    def run_forward(wave_in, patch_set, measured):
        return forward_slices(wave_in, patch_set, measured, optics, last_cut)

    def blank_forward(wave_in, patch_set, measured):
        return (jnp.zeros(patch_set.shape, jnp.bfloat16), jnp.zeros_like(wave_in))

    def run_adjoint(arriving, stored_set, patch_set):
        return adjoint_slices(arriving, stored_set, patch_set, optics)

    def blank_adjoint(arriving, stored_set, patch_set):
        return (jnp.zeros(patch_set.shape, jnp.float32), jnp.zeros_like(arriving))

    incoming = illumination
    stored_all = jnp.zeros(patches.shape, jnp.bfloat16)
    outgoing = jnp.zeros(illumination.shape, jnp.bfloat16)
    for section_index in range(cut_count):
        active = cut_index == section_index
        stored_now, outgoing = lax.cond(
            active, run_forward, blank_forward, incoming, patches, amplitudes
        )
        stored_all = jnp.where(active, stored_now, stored_all)
        if section_index < cut_count - 1:
            passed = from_behind(outgoing, "cuts", 1)
            incoming = jnp.where(first_cut, illumination, passed)
    arriving = outgoing
    pieces = jnp.zeros(patches.shape, jnp.float32)
    for section_index in reversed(range(cut_count)):
        active = cut_index == section_index
        pieces_now, backward = lax.cond(
            active, run_adjoint, blank_adjoint, arriving, stored_all, patches
        )
        pieces = jnp.where(active, pieces_now, pieces)
        if section_index > 0:
            arriving = from_behind(backward, "cuts", -1)
    gradient_ext = add_patches(
        jnp.zeros(extended.shape, jnp.float32), pieces, scan_rows, scan_cols, rim_depth
    )
    rim_pair = jnp.stack(
        [gradient_ext[:, :, :rim_depth], gradient_ext[:, :, band_rows + rim_depth :]]
    )
    received = padded(rim_pair.astype(jnp.bfloat16), (("region", 0),), 1).astype(rim_pair.dtype)
    interior = gradient_ext[:, :, rim_depth : band_rows + rim_depth]
    interior = interior.at[:, :, :rim_depth].add(received[0])
    interior = interior.at[:, :, band_rows - rim_depth :].add(received[3])
    return interior


def solution(mesh):
    return jax.shard_map(
        shards,
        mesh=mesh,
        in_specs=(
            P("cuts", None, "region", None),
            P(),
            P("region", None, None),
            P(),
            P("region"),
            P("region"),
            P("region"),
        ),
        out_specs=P("cuts", None, "region", None),
        check_vma=False,
    )
```

profile of v0, /device:TPU:1, one launch (start us, length us, event | category | flops | bytes accessed | tf_op | source)
XLA Modules:
  0.0 213.7 jit_solution(4507537664480816327)
XLA Ops:
  0.0 3.1 %fusion.97 = (f32[1,2,128,1024]{3,2,1,0:T(8,128)}, f32[1,2,128,1024]{3,2,1,0:T(8,128)}) fusion(f32[1,2,256,1024]{3,2,1,0:T(8,128)} %param.21), kind=kLoop, calls=%fused_computation.151 | loop fusion | bytes 4194304 | tf_op jit(solution)/shard_map/slice | solution.py:16
  3.2 2.6 %collective-permute-start = (f32[1,2,128,1024]{3,2,1,0:T(8,128)}, f32[1,2,128,1024]{3,2,1,0:T(8,128)}, u32[]{:S(2)}, u32[]{:S(2)}) collective-permute-start(f32[1,2,128,1024]{3,2,1,0:T(8,128)} %get-tuple-element.388), channel_id=1, source_target_pairs={{0,1},{1,2},{2,3},{3,4},{4,5},{5,6},{6,7},{7,8},{8,9},{9,10},{10,1... | collective-permute-start | bytes 3145736 | tf_op jit(solution)/shard_map/ppermute | solution.py:15
  18.7 2.3 %select_reduce_fusion = bf16[4,2,256,256]{3,2,1,0:T(8,128)(2,1)S(1)} fusion(pred[4,4]{1,0:T(4,128)(4,1)S(1)} %iota_compare_fusion, bf16[4,2,256,256]{3,2,1,0:T(8,128)(2,1)} %param.22), kind=kLoop, calls=%fused_computation.91 | loop fusion | flops 3670016 | bytes 2097168 | tf_op jit(solution)/shard_map/reduce_sum | solution.py:144
  21.0 8.0 %collective-permute-done = f32[1,2,128,1024]{3,2,1,0:T(8,128)} collective-permute-done((f32[1,2,128,1024]{3,2,1,0:T(8,128)}, f32[1,2,128,1024]{3,2,1,0:T(8,128)}, u32[]{:S(2)}, u32[]{:S(2)}) %collective-permute-start) | collective-permute-done | bytes 1048608 | tf_op jit(solution)/shard_map/ppermute | solution.py:15
  29.1 2.5 %collective-permute-done.1 = f32[1,2,128,1024]{3,2,1,0:T(8,128)} collective-permute-done((f32[1,2,128,1024]{3,2,1,0:T(8,128)}, f32[1,2,128,1024]{3,2,1,0:T(8,128)}, u32[]{:S(2)}, u32[]{:S(2)}) %collective-permute-start.1) | collective-permute-done | bytes 1048608 | tf_op jit(solution)/shard_map/ppermute | solution.py:18
  31.5 4.0 %pad_maximum_fusion = f32[1,2,512,1024]{3,2,1,0:T(8,128)} fusion(f32[1,2,128,1024]{3,2,1,0:T(8,128)} %collective-permute-done.1, f32[1,2,256,1024]{3,2,1,0:T(8,128)S(1)} %copy-done.3, f32[1,2,128,1024]{3,2,1,0:T(8,128)} %collective-permute-done), kind=kLoop, calls=%fused_computation.90 | loop fusion | flops 2097152 | bytes 8388608 | tf_op jit(solution)/shard_map/concatenate | solution.py:19
  35.6 13.6 %while.21 = (s32[]{:T(128)}, f32[1,2,512,1024]{3,2,1,0:T(8,128)}, s32[4,4]{1,0:T(4,128)S(1)}, f32[4,1,2,256,256]{4,3,2,1,0:T(8,128)S(1)}) while((s32[]{:T(128)}, f32[1,2,512,1024]{3,2,1,0:T(8,128)}, s32[4,4]{1,0:T(4,128)S(1)}, f32[4,1,2,256,256]{4,3,2,1,0:T(8,128)S(1)}) %tuple.130), condition=%wide.while_cond.2.clone, body=%wide.while_body.2.sunk.clone | while | flops 2 | bytes 1048701 | solution.py:121
  36.2 2.7 %bitcast_dynamic-update-slice_fusion.3 = f32[4,1,2,256,256]{4,3,2,1,0:T(8,128)S(1)} fusion(f32[4,1,2,256,256]{4,3,2,1,0:T(8,128)S(1)} %get-tuple-element.503, s32[]{:T(128)S(6)} %copy.76, f32[1,2,512,1024]{3,2,1,0:T(8,128)} %get-tuple-element.505, s32[]{:T(128)} %bitcast.320, s32[]{:T(128)} %bitcast.321), kind=kLoop, calls=%fused_computation.88.clone.1.clone | loop fusion | bytes 1048588 | tf_op jit(solution)/shard_map/vmap()/gather
  39.6 2.7 %bitcast_dynamic-update-slice_fusion.3 = f32[4,1,2,256,256]{4,3,2,1,0:T(8,128)S(1)} fusion(f32[4,1,2,256,256]{4,3,2,1,0:T(8,128)S(1)} %get-tuple-element.503, s32[]{:T(128)S(6)} %copy.76, f32[1,2,512,1024]{3,2,1,0:T(8,128)} %get-tuple-element.505, s32[]{:T(128)} %bitcast.320, s32[]{:T(128)} %bitcast.321), kind=kLoop, calls=%fused_computation.88.clone.1.clone | loop fusion | bytes 1048588 | tf_op jit(solution)/shard_map/vmap()/gather
  43.0 2.7 %bitcast_dynamic-update-slice_fusion.3 = f32[4,1,2,256,256]{4,3,2,1,0:T(8,128)S(1)} fusion(f32[4,1,2,256,256]{4,3,2,1,0:T(8,128)S(1)} %get-tuple-element.503, s32[]{:T(128)S(6)} %copy.76, f32[1,2,512,1024]{3,2,1,0:T(8,128)} %get-tuple-element.505, s32[]{:T(128)} %bitcast.320, s32[]{:T(128)} %bitcast.321), kind=kLoop, calls=%fused_computation.88.clone.1.clone | loop fusion | bytes 1048588 | tf_op jit(solution)/shard_map/vmap()/gather
  46.4 2.7 %bitcast_dynamic-update-slice_fusion.3 = f32[4,1,2,256,256]{4,3,2,1,0:T(8,128)S(1)} fusion(f32[4,1,2,256,256]{4,3,2,1,0:T(8,128)S(1)} %get-tuple-element.503, s32[]{:T(128)S(6)} %copy.76, f32[1,2,512,1024]{3,2,1,0:T(8,128)} %get-tuple-element.505, s32[]{:T(128)} %bitcast.320, s32[]{:T(128)} %bitcast.321), kind=kLoop, calls=%fused_computation.88.clone.1.clone | loop fusion | bytes 1048588 | tf_op jit(solution)/shard_map/vmap()/gather
  49.1 16.2 %conditional.4 = (bf16[4,1,2,256,256]{4,3,2,0,1:T(8,128)(2,1)}, bf16[4,2,256,256]{3,2,1,0:T(8,128)(2,1)}) conditional(s32[]{:T(128)} %convert_element_type.194, () %tuple.67, (bf16[4,2,256,256]{3,2,1,0:T(8,128)(2,1)S(1)}, pred[]{:T(512)}, f32[4,1,2,256,256]{4,3,2,1,0:T(8,128)S(1)}, bf16[2,2,256,256]{3,2,1,0:T(8,128)(2,1)}, ...), branch_computations={%region_1.2_spmd, %region_2.3_spmd} | conditional | flops 2160590848 | bytes 41418824 | solution.py:183
  51.9 4.1 %convolution_bitcast_fusion = f32[4,2,256,256]{3,2,1,0:T(8,128)} fusion(bf16[4,1,256,256]{3,2,1,0:T(8,128)(2,1)} %get-tuple-element.367, bf16[4,1,256,256]{3,2,1,0:T(8,128)(2,1)} %get-tuple-element.366, bf16[2,2,256,256]{3,2,1,0:T(8,128)(2,1)} %get-tuple-element.228, bf16[2,2,256,256]{3,2,1,0:T(8,128)(2,1)} %get-tuple-element.321), kind=kOutput, calls=%fused_computation.5 | convolution fusion | flops 1076363264 | bytes 4194304 | tf_op jit(solution)/shard_map/cond/branch_1_fun/nckl,cdlm->ndkm/dot_general | solution.py:57
  56.1 3.0 %multiply_subtract_fusion = (bf16[4,1,256,256]{3,2,1,0:T(8,128)(2,1)}, bf16[4,1,256,256]{3,2,1,0:T(8,128)(2,1)}) fusion(f32[4,2,256,256]{3,2,1,0:T(8,128)} %convolution_bitcast_fusion, f32[256,256]{1,0:T(8,128)S(1)} %bitcast.328, f32[256,256]{1,0:T(8,128)} %bitcast.331), kind=kLoop, calls=%fused_computation.16 | loop fusion | flops 2097152 | bytes 3670016 | tf_op jit(solution)/shard_map/cond/branch_1_fun/sub | solution.py:62
  60.5 4.8 %fusion.3 = bf16[4,2,256,256]{3,2,1,0:T(8,128)(2,1)} fusion(bf16[4,1,256,256]{3,2,1,0:T(8,128)(2,1)} %get-tuple-element.369, bf16[4,1,256,256]{3,2,1,0:T(8,128)(2,1)} %get-tuple-element.368, f32[4,2,256,256]{3,2,1,0:T(8,128)} %convolution_bitcast_fusion, f32[4,256,256]{2,1,0:T(8,128)} %fusion.10, pred[]{:T(512)} %get-tuple-element.226, ...), kind=kOutput, calls=%fused_computation.8 | convolution fusion | flops 1077936128 | bytes 6291457 | tf_op jit(solution)/shard_map/cond/branch_1_fun/nckl,cdlm->ndkm/dot_general | solution.py:57
  65.4 2.3 %collective-permute-start.2 = (bf16[4,2,256,256]{3,2,1,0:T(8,128)(2,1)}, bf16[4,2,256,256]{3,2,1,0:T(8,128)(2,1)}, u32[]{:S(2)}, u32[]{:S(2)}) collective-permute-start(bf16[4,2,256,256]{3,2,1,0:T(8,128)(2,1)} %get-tuple-element.271), channel_id=1, source_target_pairs={{0,16},{1,17},{2,18},{3,19},{4,20},{5,21},{6,22},{7,23},{8,24},{9,... | collective-permute-start | bytes 3145736 | tf_op jit(solution)/shard_map/ppermute | solution.py:26
  67.6 14.9 %collective-permute-done.2 = bf16[4,2,256,256]{3,2,1,0:T(8,128)(2,1)} collective-permute-done((bf16[4,2,256,256]{3,2,1,0:T(8,128)(2,1)}, bf16[4,2,256,256]{3,2,1,0:T(8,128)(2,1)}, u32[]{:S(2)}, u32[]{:S(2)}) %collective-permute-start.2) | collective-permute-done | bytes 1048608 | tf_op jit(solution)/shard_map/ppermute | solution.py:26
  84.6 1.7 fusion.74
  89.0 47.7 %collective-permute-done.3 = bf16[4,2,256,256]{3,2,1,0:T(8,128)(2,1)S(1)} collective-permute-done((bf16[4,2,256,256]{3,2,1,0:T(8,128)(2,1)}, bf16[4,2,256,256]{3,2,1,0:T(8,128)(2,1)S(1)}, u32[]{:S(2)}, u32[]{:S(2)}) %collective-permute-start.3) | collective-permute-done | bytes 1048608 | tf_op jit(solution)/shard_map/ppermute | solution.py:26
  136.7 4.5 %conditional.7 = (f32[4,1,2,256,256]{4,3,2,0,1:T(8,128)}) conditional(s32[]{:T(128)} %convert_element_type.194, () %tuple.65, (bf16[4,1,2,256,256]{4,3,2,1,0:T(8,128)(2,1)S(1)}, bf16[4,2,256,256]{3,2,1,0:T(8,128)(2,1)S(1)}) %tuple.72), branch_computations={%region_7.8_spmd, %region_8.9_spmd} | conditional | flops 3145728 | bytes 20971556 | solution.py:194
  141.2 2.5 %fusion.70 = f32[4,1,2,256,256]{4,3,2,1,0:T(8,128)S(1)} fusion(f32[4,1,2,256,256]{4,3,2,0,1:T(8,128)} %copy-done.2, f32[4,1,2,256,256]{4,3,2,0,1:T(8,128)} %get-tuple-element.541, pred[]{:T(512)} %eq.31, pred[]{:T(512)} %eq.30), kind=kLoop, calls=%fused_computation.93 | loop fusion | flops 1048576 | bytes 6291458 | tf_op jit(solution)/shard_map/jit(_where)/select_n | solution.py:197
  143.7 2.5 %broadcast_in_dim.27 = f32[1,2,512,1024]{3,2,1,0:T(8,128)} broadcast(f32[]{:T(128)} %constant.175.clone.1), dimensions={} | broadcast | bytes 4194308 | tf_op jit(solution)/shard_map/broadcast_in_dim | solution.py:201
  146.2 48.5 %while.20 = (s32[]{:T(128)}, f32[1,2,512,1024]{3,2,1,0:T(8,128)}, s32[4]{0:T(128)S(1)}, s32[4]{0:T(128)S(1)}, f32[4,1,2,256,256]{4,3,2,1,0:T(8,128)S(1)}, /*index=5*/s32[1]{0:T(128)}, s32[1]{0:T(128)}) while((s32[]{:T(128)}, f32[1,2,512,1024]{3,2,1,0:T(8,128)}, s32[4]{0:T(128)S(1)}, s32[4]{0:T(128)S(1)}, ...), condition=%wide.region_10.11_spmd.clone, body=%wide.region_9.10_spmd.sunk.clone | while | flops 131081 | bytes 2621645 | solution.py:138
  152.0 6.7 %dynamic_update_slice.12 = f32[1,2,512,1024]{3,2,1,0:T(8,128)} dynamic-update-slice(f32[1,2,512,1024]{3,2,1,0:T(8,128)} %get-tuple-element.528, f32[1,2,256,256]{3,2,1,0:T(8,128)S(1)} %bitcast_add_fusion.3, s32[]{:T(128)} %constant.174.clone.1..sunk.1, s32[]{:T(128)} %constant.174.clone.1..sunk.1, s32[]{:T(128)S(6)} %select_n.242, s32[]{:T(128)S(6)} %select_n.243) | dynamic-update-slice | bytes 1048580 | tf_op jit(solution)/shard_map/while/body/eval_jaxpr/dynamic_update_slice | solution.py:136
  164.5 6.7 %dynamic_update_slice.12 = f32[1,2,512,1024]{3,2,1,0:T(8,128)} dynamic-update-slice(f32[1,2,512,1024]{3,2,1,0:T(8,128)} %get-tuple-element.528, f32[1,2,256,256]{3,2,1,0:T(8,128)S(1)} %bitcast_add_fusion.3, s32[]{:T(128)} %constant.174.clone.1..sunk.1, s32[]{:T(128)} %constant.174.clone.1..sunk.1, s32[]{:T(128)S(6)} %select_n.242, s32[]{:T(128)S(6)} %select_n.243) | dynamic-update-slice | bytes 1048580 | tf_op jit(solution)/shard_map/while/body/eval_jaxpr/dynamic_update_slice | solution.py:136
  176.9 6.0 %dynamic_update_slice.12 = f32[1,2,512,1024]{3,2,1,0:T(8,128)} dynamic-update-slice(f32[1,2,512,1024]{3,2,1,0:T(8,128)} %get-tuple-element.528, f32[1,2,256,256]{3,2,1,0:T(8,128)S(1)} %bitcast_add_fusion.3, s32[]{:T(128)} %constant.174.clone.1..sunk.1, s32[]{:T(128)} %constant.174.clone.1..sunk.1, s32[]{:T(128)S(6)} %select_n.242, s32[]{:T(128)S(6)} %select_n.243) | dynamic-update-slice | bytes 1048580 | tf_op jit(solution)/shard_map/while/body/eval_jaxpr/dynamic_update_slice | solution.py:136
  188.7 6.0 %dynamic_update_slice.12 = f32[1,2,512,1024]{3,2,1,0:T(8,128)} dynamic-update-slice(f32[1,2,512,1024]{3,2,1,0:T(8,128)} %get-tuple-element.528, f32[1,2,256,256]{3,2,1,0:T(8,128)S(1)} %bitcast_add_fusion.3, s32[]{:T(128)} %constant.174.clone.1..sunk.1, s32[]{:T(128)} %constant.174.clone.1..sunk.1, s32[]{:T(128)S(6)} %select_n.242, s32[]{:T(128)S(6)} %select_n.243) | dynamic-update-slice | bytes 1048580 | tf_op jit(solution)/shard_map/while/body/eval_jaxpr/dynamic_update_slice | solution.py:136
  194.7 1.7 fusion.96
  196.5 1.7 collective-permute-start.4
  198.2 1.8 slice.229
  200.1 8.5 %collective-permute-done.5 = bf16[1,1,2,128,1024]{4,3,2,1,0:T(8,128)(2,1)S(1)} collective-permute-done((bf16[1,1,2,128,1024]{4,3,2,1,0:T(8,128)(2,1)S(1)}, bf16[1,1,2,128,1024]{4,3,2,1,0:T(8,128)(2,1)S(1)}, u32[]{:S(2)}, u32[]{:S(2)}) %collective-permute-start.5) | collective-permute-done | bytes 524320 | tf_op jit(solution)/shard_map/ppermute | solution.py:18
  211.4 2.4 %fusion.71 = f32[1,2,256,1024]{3,2,1,0:T(8,128)} fusion(f32[1,2,256,1024]{3,2,1,0:T(8,128)} %copy-done.4, bf16[1,1,2,128,1024]{4,3,2,1,0:T(8,128)(2,1)S(1)} %collective-permute-done.5, bf16[2,1,2,128,1024]{4,3,2,1,0:T(8,128)(2,1)S(1)} %maximum_bitcast_fusion.18, bf16[1,1,2,128,1024]{4,3,2,1,0:T(8,128)(2,1)S(1)} %collective-permute-done.4), kind=kLoop, calls=%fused_computation.95 | loop fusion | flops 1835008 | bytes 4194304 | tf_op jit(solution)/shard_map/scatter-add | solution.py:209
  (86 shorter events, 44.2 us)
Async XLA Ops:
  0.0 13.7 %copy-start.15 = (s32[4]{0:T(128)S(1)}, s32[4]{0:T(128)}, u32[]{:S(2)}) copy-start(s32[4]{0:T(128)} %param.26) | copy-start | bytes 52
  0.0 13.7 %copy-start.14 = (s32[4]{0:T(128)S(1)}, s32[4]{0:T(128)}, u32[]{:S(2)}) copy-start(s32[4]{0:T(128)} %param.25) | copy-start | bytes 52
  3.2 25.9 %collective-permute-start = (f32[1,2,128,1024]{3,2,1,0:T(8,128)}, f32[1,2,128,1024]{3,2,1,0:T(8,128)}, u32[]{:S(2)}, u32[]{:S(2)}) collective-permute-start(f32[1,2,128,1024]{3,2,1,0:T(8,128)} %get-tuple-element.388), channel_id=1, source_target_pairs={{0,1},{1,2},{2,3},{3,4},{4,5},{5,6},{6,7},{7,8},{8,9},{9,10},{10,1... | collective-permute-start | bytes 3145736 | tf_op jit(solution)/shard_map/ppermute | solution.py:15
  5.8 25.8 %collective-permute-start.1 = (f32[1,2,128,1024]{3,2,1,0:T(8,128)}, f32[1,2,128,1024]{3,2,1,0:T(8,128)}, u32[]{:S(2)}, u32[]{:S(2)}) collective-permute-start(f32[1,2,128,1024]{3,2,1,0:T(8,128)} %get-tuple-element.389), channel_id=1, source_target_pairs={{1,0},{2,1},{3,2},{4,3},{5,4},{6,5},{7,6},{8,7},{9,8},{10,9},{11,1... | collective-permute-start | bytes 3145736 | tf_op jit(solution)/shard_map/ppermute | solution.py:18
  13.9 3.1 %copy-start.16 = (s32[4]{0:T(128)S(1)}, s32[4]{0:T(128)}, u32[]{:S(2)}) copy-start(s32[4]{0:T(128)} %param.27) | copy-start | bytes 52
  13.9 3.2 %copy-start.13 = (f32[256,256]{1,0:T(8,128)S(1)}, f32[256,256]{1,0:T(8,128)}, u32[]{:S(2)}) copy-start(f32[256,256]{1,0:T(8,128)} %param.24) | copy-start | bytes 786436
  17.0 14.6 %copy-start.3 = (f32[1,2,256,1024]{3,2,1,0:T(8,128)S(1)}, f32[1,2,256,1024]{3,2,1,0:T(8,128)}, u32[]{:S(2)}) copy-start(f32[1,2,256,1024]{3,2,1,0:T(8,128)} %param.21) | copy-start | bytes 6291460
  56.1 3.0 %copy-start = (f32[4,2,256,256]{3,2,1,0:T(8,128)S(1)}, f32[4,2,256,256]{3,2,1,0:T(8,128)}, u32[]{:S(2)}) copy-start(f32[4,2,256,256]{3,2,1,0:T(8,128)} %convolution_bitcast_fusion) | copy-start | bytes 6291460 | tf_op jit(solution)/shard_map/cond
  56.1 3.0 %copy-start.9 = (f32[4,256,256]{2,1,0:T(8,128)S(1)}, f32[4,256,256]{2,1,0:T(8,128)}, u32[]{:S(2)}) copy-start(f32[4,256,256]{2,1,0:T(8,128)} %get-tuple-element.230) | copy-start | bytes 3145732 | tf_op jit(solution)/shard_map/cond
  65.4 17.2 %collective-permute-start.2 = (bf16[4,2,256,256]{3,2,1,0:T(8,128)(2,1)}, bf16[4,2,256,256]{3,2,1,0:T(8,128)(2,1)}, u32[]{:S(2)}, u32[]{:S(2)}) collective-permute-start(bf16[4,2,256,256]{3,2,1,0:T(8,128)(2,1)} %get-tuple-element.271), channel_id=1, source_target_pairs={{0,16},{1,17},{2,18},{3,19},{4,20},{5,21},{6,22},{7,23},{8,24},{9,... | collective-permute-start | bytes 3145736 | tf_op jit(solution)/shard_map/ppermute | solution.py:26
  83.6 1.0 copy-start.7
  84.6 1.9 copy-start.8
  87.7 49.0 %copy-start.2 = (f32[4,1,2,256,256]{4,3,2,0,1:T(8,128)}, f32[4,1,2,256,256]{4,3,2,0,1:T(8,128)S(1)}, u32[]{:S(2)}) copy-start(f32[4,1,2,256,256]{4,3,2,0,1:T(8,128)S(1)} %get-tuple-element.276) | copy-start | bytes 6291460
  87.7 49.0 %collective-permute-start.3 = (bf16[4,2,256,256]{3,2,1,0:T(8,128)(2,1)}, bf16[4,2,256,256]{3,2,1,0:T(8,128)(2,1)S(1)}, u32[]{:S(2)}, u32[]{:S(2)}) collective-permute-start(bf16[4,2,256,256]{3,2,1,0:T(8,128)(2,1)} %get-tuple-element.275), channel_id=1, source_target_pairs={{16,0},{17,1},{18,2},{19,3},{20,4},{21,5},{22,6},{23,7},{24,8},{25... | collective-permute-start | bytes 3145736 | tf_op jit(solution)/shard_map/ppermute | solution.py:26
  136.7 1.0 copy-start.11
  196.4 12.2 %collective-permute-start.5 = (bf16[1,1,2,128,1024]{4,3,2,1,0:T(8,128)(2,1)S(1)}, bf16[1,1,2,128,1024]{4,3,2,1,0:T(8,128)(2,1)S(1)}, u32[]{:S(2)}, u32[]{:S(2)}) collective-permute-start(bf16[1,1,2,128,1024]{4,3,2,1,0:T(8,128)(2,1)S(1)} %bitcast.335), channel_id=1, source_target_pairs={{1,0},{2,1},{3,2},{4,3},{5,4},{6,5},{7,6},{8,7},{9,8},{10,9},{11,1... | collective-permute-start | bytes 1572872 | tf_op jit(solution)/shard_map/ppermute | solution.py:18
  196.5 12.2 %collective-permute-start.4 = (bf16[1,1,2,128,1024]{4,3,2,1,0:T(8,128)(2,1)S(1)}, bf16[1,1,2,128,1024]{4,3,2,1,0:T(8,128)(2,1)S(1)}, u32[]{:S(2)}, u32[]{:S(2)}) collective-permute-start(bf16[1,1,2,128,1024]{4,3,2,1,0:T(8,128)(2,1)S(1)} %bitcast.334), channel_id=1, source_target_pairs={{0,1},{1,2},{2,3},{3,4},{4,5},{5,6},{6,7},{7,8},{8,9},{9,10},{10,1... | collective-permute-start | bytes 1572872 | tf_op jit(solution)/shard_map/ppermute | solution.py:15
  210.0 1.3 copy-start.4
where the time goes:
time: 216 us; the launch traced here: 214 us
  waiting for transfers between devices  81.5 us (38%)
  local copies, waits for them, and re-layouts  61.2 us (28%)
  other arithmetic  40.5 us (19%)
  loops' own time  13.3 us (6%)
  matrix products  8.93 us (4%)
  starting transfers between devices  7.98 us (4%)
    ppermute x2, waiting for transfers between devices, from_behind(): return lax.ppermute(block, axis, route)  62.6 us
    dynamic_update_slice x4, local copies, waits for them, and re-layouts, deposit(): lax.dynamic_update_slice(running, existing + pieces[position], corner)  25.4 us
    gather x12, local copies, waits for them, and re-layouts  13.5 us
    another operation x1, loops' own time, add_patches(): return lax.fori_loop(0, pieces.shape[0], deposit, gradient)  13 us
    ppermute x2, waiting for transfers between devices, padded(): lax.ppermute(lax.slice_in_dim(block, 0, width, axis=dim), axis, backward)  11 us
    dot_general x2, matrix products, transform(): jnp.einsum('nckl,cdlm->ndkm', middle, right_block, preferred_element_type...  8.93 us
    ppermute x2, waiting for transfers between devices, padded(): lax.ppermute(lax.slice_in_dim(block, block.shape[dim] - width, None, axis...  8.02 us
    add x4, other arithmetic, deposit(): existing + pieces[position]  5.49 us
  transfers between devices with their start and end apart: 6, of which 5 were waited for; matrix products, arithmetic and copies ran while one was open for 8% of the time, Pallas kernels for 0%

commit v1 on v0

v1 whole, which is shorter than its diff:
```python
import functools
import jax
import jax.numpy as jnp
import numpy as np
from jax import lax
from jax.experimental import pallas as pl
from jax.experimental.pallas import tpu as pltpu
from jax.sharding import PartitionSpec as P

modulus_floor = 0.25
LANES = 128
SUBLANES = 8
VMEM = pl.BlockSpec(memory_space=pltpu.VMEM)
SMEM = pl.BlockSpec(memory_space=pltpu.SMEM)
LIMIT = pltpu.CompilerParams(vmem_limit_bytes=60000 * 1024)


def dft_blocks(side):
    indices = np.arange(side)
    angles = (indices[:, None] * indices[None, :] % side) * (2.0 * np.pi / side)
    real = np.cos(angles) / np.sqrt(side)
    imag = np.sin(angles) / np.sqrt(side)
    tables = []
    for sign in (-1.0, 1.0):
        tables.append(np.block([[real, -sign * imag], [sign * imag, real]]))
        tables.append(np.block([[real, sign * imag], [-sign * imag, real]]))
    return jnp.asarray(np.stack(tables), dtype=jnp.bfloat16)


def split_col(col, cols, side):
    base = jnp.minimum(col // LANES, (cols - side) // LANES - 1) * LANES
    return pl.multiple_of(base, LANES), col - base


def cut_window(ext, plane, row, col, side):
    base, shift = split_col(col, ext.shape[2], side)
    top = pl.multiple_of(row // SUBLANES * SUBLANES, SUBLANES)
    tall = side + SUBLANES
    block = ext[plane, pl.ds(top, tall), pl.ds(base, side + LANES)]
    block = pltpu.roll(block, lax.rem(tall + top - row, tall), axis=0)[:side]
    back = lax.rem(LANES - shift + LANES, LANES)
    chunks = [
        pltpu.roll(block[:, j : j + LANES], back, axis=1) for j in range(0, side + LANES, LANES)
    ]
    lane = lax.broadcasted_iota(jnp.int32, (side, LANES), 1)
    keep = lane < LANES - shift
    return jnp.concatenate(
        [jnp.where(keep, chunks[j], chunks[j + 1]) for j in range(len(chunks) - 1)], axis=1
    )


def add_window(grad, plane, row, col, field):
    side = field.shape[0]
    base, shift = split_col(col, grad.shape[2], side)
    top = pl.multiple_of(row // SUBLANES * SUBLANES, SUBLANES)
    tall = side + SUBLANES
    field = jnp.concatenate([field, jnp.zeros((SUBLANES, side), field.dtype)], axis=0)
    field = pltpu.roll(field, row - top, axis=0)
    ahead = lax.rem(shift, LANES)
    chunks = [pltpu.roll(field[:, j : j + LANES], ahead, axis=1) for j in range(0, side, LANES)]
    lane = lax.broadcasted_iota(jnp.int32, (tall, LANES), 1)
    keep = lane >= shift
    zero = jnp.zeros((tall, LANES), field.dtype)
    parts = [zero] + chunks + [zero]
    placed = jnp.concatenate(
        [jnp.where(keep, parts[j + 1], parts[j]) for j in range(len(chunks) + 1)], axis=1
    )
    where = (plane, pl.ds(top, tall), pl.ds(base, side + LANES))
    grad[where] = grad[where] + placed


def cut_kernel(side, half, rows, cols, cut, band, low, high, own, sent, ext):
    rim = low.shape[1]
    band_rows = band.shape[1]
    ext[:, :rim] = low[...].astype(jnp.float32)
    ext[:, rim : rim + band_rows] = band[...]
    ext[:, rim + band_rows : 2 * rim + band_rows] = high[...].astype(jnp.float32)
    for index in range(half):
        for target, first in ((own, cut[0] * half), (sent, (1 - cut[0]) * half)):
            position = first + index
            for plane in range(2):
                target[index, plane] = cut_window(
                    ext, plane, rows[position] + rim, cols[position], side
                ).astype(target.dtype)


def dot(left, right):
    return jnp.dot(left, right, preferred_element_type=jnp.float32)


def transform(field, tables, which):
    side = field[0].shape[0]
    stacked = jnp.concatenate([field[0].astype(jnp.bfloat16), field[1].astype(jnp.bfloat16)], axis=0)
    middle = dot(tables[which], stacked).astype(jnp.bfloat16)
    beside = jnp.concatenate([middle[:side], middle[side:]], axis=1)
    result = dot(beside, tables[which + 1])
    return result[:, :side], result[:, side:]


def multiply(left, right):
    return left[0] * right[0] - left[1] * right[1], left[0] * right[1] + left[1] * right[0]


def multiply_conjugate(left, right):
    return left[0] * right[0] + left[1] * right[1], left[0] * right[1] - left[1] * right[0]


def narrowed(field):
    return tuple(part.astype(jnp.bfloat16).astype(jnp.float32) for part in field)


def one_position(psi0, object0, object1, measured, wave, tables):
    psi1 = narrowed(
        transform(multiply(wave, transform(multiply(psi0, object0), tables, 0)), tables, 2)
    )
    far = transform(multiply(psi1, object1), tables, 0)
    modulus = jnp.sqrt(far[0] * far[0] + far[1] * far[1])
    factor = 1.0 - measured / jnp.maximum(modulus, modulus_floor)
    g1 = narrowed(transform((far[0] * factor, far[1] * factor), tables, 2))
    d1 = multiply_conjugate(psi1, g1)
    back = transform(multiply_conjugate(object1, g1), tables, 0)
    g0 = narrowed(transform(multiply_conjugate(wave, back), tables, 2))
    return multiply_conjugate(psi0, g0), d1


def wide(ref, *index):
    return ref[index + (0,)].astype(jnp.float32), ref[index + (1,)].astype(jnp.float32)


def wave_kernel(half, choice, cut, own, other, probes, amps, wave, tables, mine, theirs):
    c = cut[0]
    first = c == 0
    for index in range(half):
        position = c * half + index
        psi0 = wide(probes, choice[position])
        a = wide(own, index)
        b = wide(other, index)
        object0 = tuple(jnp.where(first, x, y) for x, y in zip(a, b))
        object1 = tuple(jnp.where(first, y, x) for x, y in zip(a, b))
        d0, d1 = one_position(psi0, object0, object1, amps[position], (wave[0], wave[1]), tables)
        for plane in range(2):
            mine[index, plane] = jnp.where(first, d0[plane], d1[plane]).astype(mine.dtype)
            theirs[index, plane] = jnp.where(first, d1[plane], d0[plane]).astype(theirs.dtype)


def deposit_kernel(half, rows, cols, cut, mine, arrived, inner, low, high, grad):
    rim = low.shape[1]
    band_rows = inner.shape[1]
    grad[...] = jnp.zeros_like(grad)
    for index in range(half):
        for source, first in ((mine, cut[0] * half), (arrived, (1 - cut[0]) * half)):
            position = first + index
            for plane in range(2):
                add_window(
                    grad, plane, rows[position] + rim, cols[position],
                    source[index, plane].astype(jnp.float32),
                )
    low[...] = grad[:, :rim].astype(low.dtype)
    inner[...] = grad[:, rim : rim + band_rows]
    high[...] = grad[:, rim + band_rows : 2 * rim + band_rows].astype(high.dtype)


def shards(objects, probes, amplitudes, prop_phase, scan_rows, scan_cols, probe_choice):
    side = probes.shape[-1]
    rim = side // 2
    count = lax.axis_size("region")
    band = objects[0]
    band_rows, columns = band.shape[1:]
    half = scan_rows.shape[0] // 2
    cut = lax.axis_index("cuts").astype(jnp.int32)[None]
    forward = [(i, (i + 1) % count) for i in range(count)]
    backward = [(i, (i - 1) % count) for i in range(count)]
    swap = [(0, 1), (1, 0)]
    low = lax.ppermute(band[:, band_rows - rim :].astype(jnp.bfloat16), "region", forward)
    high = lax.ppermute(band[:, :rim].astype(jnp.bfloat16), "region", backward)
    wave = jnp.stack([jnp.cos(prop_phase), jnp.sin(prop_phase)])
    tables = dft_blocks(side)
    fields = jax.ShapeDtypeStruct((half, 2, side, side), jnp.bfloat16)
    tall = pltpu.VMEM((2, band_rows + 2 * rim + SUBLANES, columns), jnp.float32)
    own, sent = pl.pallas_call(
        functools.partial(cut_kernel, side, half),
        out_shape=(fields, fields),
        in_specs=[SMEM] * 3 + [VMEM] * 3,
        out_specs=(VMEM, VMEM),
        scratch_shapes=[tall],
        compiler_params=LIMIT,
    )(scan_rows, scan_cols, cut, band, low, high)
    other = lax.ppermute(sent, "cuts", swap)
    mine, theirs = pl.pallas_call(
        functools.partial(wave_kernel, half),
        out_shape=(fields, fields),
        in_specs=[SMEM] * 2 + [VMEM] * 6,
        out_specs=(VMEM, VMEM),
        compiler_params=LIMIT,
    )(probe_choice, cut, own, other, probes, amplitudes, wave, tables)
    arrived = lax.ppermute(theirs, "cuts", swap)
    edge = jax.ShapeDtypeStruct((2, rim, columns), jnp.bfloat16)
    inner, up, down = pl.pallas_call(
        functools.partial(deposit_kernel, half),
        out_shape=(jax.ShapeDtypeStruct(band.shape, jnp.float32), edge, edge),
        in_specs=[SMEM] * 3 + [VMEM] * 2,
        out_specs=(VMEM, VMEM, VMEM),
        scratch_shapes=[tall],
        compiler_params=LIMIT,
    )(scan_rows, scan_cols, cut, mine, arrived)
    from_above = lax.ppermute(down, "region", forward)
    from_below = lax.ppermute(up, "region", backward)
    rims = jnp.concatenate([from_above, from_below], axis=1).astype(jnp.float32)
    return (inner + rims)[None]


def solution(mesh):
    return jax.shard_map(
        shards,
        mesh=mesh,
        in_specs=(
            P("cuts", None, "region", None),
            P(),
            P("region", None, None),
            P(),
            P("region"),
            P("region"),
            P("region"),
        ),
        out_specs=P("cuts", None, "region", None),
        check_vma=False,
    )
```

time: 216 us -> 79.9 us (0.37)
  the two profiles are of different devices: /device:TPU:1 before, /device:TPU:0 now
where the time goes in v1:
time: 79.9 us; the launch traced here: 79.7 us
  waiting for transfers between devices  37.1 us (46%)
  Pallas kernels  20.2 us (25%)
  starting transfers between devices  13 us (16%)
  other arithmetic  5.98 us (7%)
  local copies, waits for them, and re-layouts  3.41 us (4%)
    pallas_call x1, Pallas kernels, shards(): pl.pallas_call(functools.partial(wave_kernel, half), out_shape=(fields, f...  11.6 us
    ppermute x1, waiting for transfers between devices, shards(): arrived = lax.ppermute(theirs, 'cuts', swap)  9.83 us
    ppermute x1, waiting for transfers between devices, shards(): other = lax.ppermute(sent, 'cuts', swap)  8.86 us
    ppermute x1, waiting for transfers between devices, shards(): from_above = lax.ppermute(down, 'region', forward)  7.07 us
    ppermute x1, waiting for transfers between devices, shards(): high = lax.ppermute(band[:, :rim].astype(jnp.bfloat16), 'region', backward)  6.7 us
    ppermute x1, starting transfers between devices, shards(): high = lax.ppermute(band[:, :rim].astype(jnp.bfloat16), 'region', backward)  5.53 us
    ppermute x1, waiting for transfers between devices, shards(): lax.ppermute(band[:, band_rows - rim:].astype(jnp.bfloat16), 'region', fo...  4.6 us
    ppermute x1, starting transfers between devices, shards(): from_below = lax.ppermute(up, 'region', backward)  4.44 us
  transfers between devices with their start and end apart: 6, of which 5 were waited for; matrix products, arithmetic and copies ran while one was open for 2% of the time, Pallas kernels for 0%

profile of v1, /device:TPU:0, one launch (start us, length us, event | category | flops | bytes accessed | tf_op | source)
XLA Modules:
  0.0 79.7 jit_solution(4301890253036971626)
XLA Ops:
  0.0 1.7 %bitcast_convert_fusion = bf16[2,256,1024]{2,1,0:T(8,128)(2,1)S(1)} fusion(f32[1,2,256,1024]{3,2,1,0:T(8,128)} %param.8), kind=kLoop, calls=%fused_computation.4 | loop fusion | flops 524288 | bytes 3145728 | tf_op jit(solution)/shard_map/convert.1
  1.8 0.1 fusion
  1.8 0.0 copy-start.4
  1.8 5.5 %collective-permute-start.1 = (bf16[2,128,1024]{2,1,0:T(8,128)(2,1)S(1)}, bf16[2,128,1024]{2,1,0:T(8,128)(2,1)S(1)}, u32[]{:S(2)}, u32[]{:S(2)}) collective-permute-start(bf16[2,128,1024]{2,1,0:T(8,128)(2,1)S(1)} %get-tuple-element.19), channel_id=1, source_target_pairs={{0,15},{1,0},{2,1},{3,2},{4,3},{5,4},{6,5},{7,6},{8,7},{9,8},{10,9... | collective-permute-start | bytes 1572872 | tf_op jit(solution)/shard_map/ppermute | solution.py:175
  7.4 0.0 collective-permute-start
  7.4 6.7 %collective-permute-done.1.high = bf16[2,128,1024]{2,1,0:T(8,128)(2,1)S(1)} collective-permute-done((bf16[2,128,1024]{2,1,0:T(8,128)(2,1)S(1)}, bf16[2,128,1024]{2,1,0:T(8,128)(2,1)S(1)}, u32[]{:S(2)}, u32[]{:S(2)}) %collective-permute-start.1) | collective-permute-done | bytes 524320 | tf_op jit(solution)/shard_map/ppermute | solution.py:175
  14.1 0.0 copy-start
  14.1 4.6 %collective-permute-done.low = bf16[2,128,1024]{2,1,0:T(8,128)(2,1)S(1)} collective-permute-done((bf16[2,128,1024]{2,1,0:T(8,128)(2,1)S(1)}, bf16[2,128,1024]{2,1,0:T(8,128)(2,1)S(1)}, u32[]{:S(2)}, u32[]{:S(2)}) %collective-permute-start) | collective-permute-done | bytes 524320 | tf_op jit(solution)/shard_map/ppermute | solution.py:174
  18.7 0.0 copy-start.1
  18.7 0.0 copy-done
  18.7 0.8 copy-done.1
  19.5 4.3 %shard_map.82 = (bf16[2,2,256,256]{3,2,1,0:T(8,128)(2,1)}, bf16[2,2,256,256]{3,2,1,0:T(8,128)(2,1)}) custom-call(s32[4]{0:T(128)} %rows.3, s32[4]{0:T(128)} %cols.3, s32[1]{0:T(128)} %bitcast.cut, f32[2,256,1024]{2,1,0:T(8,128)} %bitcast.9, bf16[2,128,1024]{2,1,0:T(8,128)(2,1)} %copy-done.1, bf16[2,128,1024]{2,1,0:T(8,128)(2,1)} %copy-done), custom_call_target="tpu_custom_call" | custom-call | tf_op jit(solution)/shard_map/pallas_call | solution.py:180
  23.7 1.5 %collective-permute-start.2 = (bf16[2,2,256,256]{3,2,1,0:T(8,128)(2,1)}, bf16[2,2,256,256]{3,2,1,0:T(8,128)(2,1)S(1)}, u32[]{:S(2)}, u32[]{:S(2)}) collective-permute-start(bf16[2,2,256,256]{3,2,1,0:T(8,128)(2,1)} %get-tuple-element.13), channel_id=1, source_target_pairs={{0,16},{16,0},{1,17},{17,1},{2,18},{18,2},{3,19},{19,3},{4,20},{20... | collective-permute-start | bytes 1572872 | tf_op jit(solution)/shard_map/ppermute | solution.py:188
  25.2 0.0 copy-done.4
  25.2 0.9 %cosine_bitcast_fusion = (f32[1,256,256]{2,1,0:T(8,128)S(1)}, f32[1,256,256]{2,1,0:T(8,128)S(1)}) fusion(f32[256,256]{1,0:T(8,128)S(1)} %copy-done.4), kind=kLoop, calls=%fused_computation.3 | loop fusion | bytes 786432 | tf_op jit(solution)/shard_map/stack | solution.py:176
  26.2 0.9 %pad_maximum_fusion.wave = f32[2,256,256]{2,1,0:T(8,128)} fusion(f32[1,256,256]{2,1,0:T(8,128)S(1)} %get-tuple-element.22, f32[1,256,256]{2,1,0:T(8,128)S(1)} %get-tuple-element.21), kind=kLoop, calls=%fused_computation.1 | loop fusion | flops 131072 | bytes 1048576 | tf_op jit(solution)/shard_map/stack | solution.py:176
  27.0 8.9 %collective-permute-done.2.other = bf16[2,2,256,256]{3,2,1,0:T(8,128)(2,1)S(1)} collective-permute-done((bf16[2,2,256,256]{3,2,1,0:T(8,128)(2,1)}, bf16[2,2,256,256]{3,2,1,0:T(8,128)(2,1)S(1)}, u32[]{:S(2)}, u32[]{:S(2)}) %collective-permute-start.2) | collective-permute-done | bytes 524320 | tf_op jit(solution)/shard_map/ppermute | solution.py:188
  35.9 0.0 copy-start.2
  35.9 0.8 copy-done.2
  36.7 11.6 %shard_map.83 = (bf16[2,2,256,256]{3,2,1,0:T(8,128)(2,1)}, bf16[2,2,256,256]{3,2,1,0:T(8,128)(2,1)}) custom-call(s32[4]{0:T(128)} %choice.1, s32[1]{0:T(128)} %bitcast.cut, bf16[2,2,256,256]{3,2,1,0:T(8,128)(2,1)} %get-tuple-element.12.own, bf16[2,2,256,256]{3,2,1,0:T(8,128)(2,1)} %copy-done.2, bf16[4,2,256,256]{3,2,1,0:T(8,128)(2,1)} %probes.1, ...), custom_call_target="tpu_custom_call" | custom-call | tf_op jit(solution)/shard_map/pallas_call | solution.py:189
  48.3 1.5 %collective-permute-start.3 = (bf16[2,2,256,256]{3,2,1,0:T(8,128)(2,1)}, bf16[2,2,256,256]{3,2,1,0:T(8,128)(2,1)S(1)}, u32[]{:S(2)}, u32[]{:S(2)}) collective-permute-start(bf16[2,2,256,256]{3,2,1,0:T(8,128)(2,1)} %get-tuple-element.15), channel_id=1, source_target_pairs={{0,16},{16,0},{1,17},{17,1},{2,18},{18,2},{3,19},{19,3},{4,20},{20... | collective-permute-start | bytes 1572872 | tf_op jit(solution)/shard_map/ppermute | solution.py:196
  49.8 9.8 %collective-permute-done.3.arrived = bf16[2,2,256,256]{3,2,1,0:T(8,128)(2,1)S(1)} collective-permute-done((bf16[2,2,256,256]{3,2,1,0:T(8,128)(2,1)}, bf16[2,2,256,256]{3,2,1,0:T(8,128)(2,1)S(1)}, u32[]{:S(2)}, u32[]{:S(2)}) %collective-permute-start.3) | collective-permute-done | bytes 524320 | tf_op jit(solution)/shard_map/ppermute | solution.py:196
  59.7 0.0 copy-start.3
  59.7 0.8 copy-done.3
  60.5 4.3 %shard_map.84 = (f32[2,256,1024]{2,1,0:T(8,128)}, bf16[2,128,1024]{2,1,0:T(8,128)(2,1)}, bf16[2,128,1024]{2,1,0:T(8,128)(2,1)}) custom-call(s32[4]{0:T(128)} %rows.3, s32[4]{0:T(128)} %cols.3, s32[1]{0:T(128)} %bitcast.cut, bf16[2,2,256,256]{3,2,1,0:T(8,128)(2,1)} %get-tuple-element.14.mine, bf16[2,2,256,256]{3,2,1,0:T(8,128)(2,1)} %copy-done.3), custom_call_target="tpu_custom_call" | custom-call | tf_op jit(solution)/shard_map/pallas_call | solution.py:198
  64.8 0.0 collective-permute-start.4
  64.8 4.4 %collective-permute-start.5 = (bf16[2,128,1024]{2,1,0:T(8,128)(2,1)}, bf16[2,128,1024]{2,1,0:T(8,128)(2,1)S(1)}, u32[]{:S(2)}, u32[]{:S(2)}) collective-permute-start(bf16[2,128,1024]{2,1,0:T(8,128)(2,1)} %get-tuple-element.18), channel_id=1, source_target_pairs={{0,15},{1,0},{2,1},{3,2},{4,3},{5,4},{6,5},{7,6},{8,7},{9,8},{10,9... | collective-permute-start | bytes 1572872 | tf_op jit(solution)/shard_map/ppermute | solution.py:207
  69.2 7.1 %collective-permute-done.4 = bf16[2,128,1024]{2,1,0:T(8,128)(2,1)S(1)} collective-permute-done((bf16[2,128,1024]{2,1,0:T(8,128)(2,1)}, bf16[2,128,1024]{2,1,0:T(8,128)(2,1)S(1)}, u32[]{:S(2)}, u32[]{:S(2)}) %collective-permute-start.4) | collective-permute-done | bytes 524320 | tf_op jit(solution)/shard_map/ppermute | solution.py:206
  76.3 0.0 collective-permute-done.5
  76.3 3.4 %add_bitcast_fusion = f32[1,2,256,1024]{3,2,1,0:T(8,128)} fusion(f32[2,256,1024]{2,1,0:T(8,128)} %get-tuple-element.16, bf16[2,128,1024]{2,1,0:T(8,128)(2,1)S(1)} %collective-permute-done.5, bf16[2,128,1024]{2,1,0:T(8,128)(2,1)S(1)} %collective-permute-done.4), kind=kLoop, calls=%fused_computation | loop fusion | flops 2621440 | bytes 5242880 | tf_op jit(solution)/shard_map/broadcast_in_dim | solution.py:209
Async XLA Ops:
  1.8 23.4 %copy-start.4 = (f32[256,256]{1,0:T(8,128)S(1)}, f32[256,256]{1,0:T(8,128)}, u32[]{:S(2)}) copy-start(f32[256,256]{1,0:T(8,128)} %param.11) | copy-start | bytes 786436
  1.8 12.2 %collective-permute-start.1 = (bf16[2,128,1024]{2,1,0:T(8,128)(2,1)S(1)}, bf16[2,128,1024]{2,1,0:T(8,128)(2,1)S(1)}, u32[]{:S(2)}, u32[]{:S(2)}) collective-permute-start(bf16[2,128,1024]{2,1,0:T(8,128)(2,1)S(1)} %get-tuple-element.19), channel_id=1, source_target_pairs={{0,15},{1,0},{2,1},{3,2},{4,3},{5,4},{6,5},{7,6},{8,7},{9,8},{10,9... | collective-permute-start | bytes 1572872 | tf_op jit(solution)/shard_map/ppermute | solution.py:175
  7.4 11.3 %collective-permute-start = (bf16[2,128,1024]{2,1,0:T(8,128)(2,1)S(1)}, bf16[2,128,1024]{2,1,0:T(8,128)(2,1)S(1)}, u32[]{:S(2)}, u32[]{:S(2)}) collective-permute-start(bf16[2,128,1024]{2,1,0:T(8,128)(2,1)S(1)} %get-tuple-element.20), channel_id=1, source_target_pairs={{0,1},{1,2},{2,3},{3,4},{4,5},{5,6},{6,7},{7,8},{8,9},{9,10},{10,1... | collective-permute-start | bytes 1572872 | tf_op jit(solution)/shard_map/ppermute | solution.py:174
  14.1 4.6 %copy-start = (bf16[2,128,1024]{2,1,0:T(8,128)(2,1)}, bf16[2,128,1024]{2,1,0:T(8,128)(2,1)S(1)}, u32[]{:S(2)}) copy-start(bf16[2,128,1024]{2,1,0:T(8,128)(2,1)S(1)} %collective-permute-done.1.high) | copy-start | bytes 1572868
  18.7 0.8 copy-start.1
  23.7 12.2 %collective-permute-start.2 = (bf16[2,2,256,256]{3,2,1,0:T(8,128)(2,1)}, bf16[2,2,256,256]{3,2,1,0:T(8,128)(2,1)S(1)}, u32[]{:S(2)}, u32[]{:S(2)}) collective-permute-start(bf16[2,2,256,256]{3,2,1,0:T(8,128)(2,1)} %get-tuple-element.13), channel_id=1, source_target_pairs={{0,16},{16,0},{1,17},{17,1},{2,18},{18,2},{3,19},{19,3},{4,20},{20... | collective-permute-start | bytes 1572872 | tf_op jit(solution)/shard_map/ppermute | solution.py:188
  35.9 0.8 copy-start.2
  48.3 11.3 %collective-permute-start.3 = (bf16[2,2,256,256]{3,2,1,0:T(8,128)(2,1)}, bf16[2,2,256,256]{3,2,1,0:T(8,128)(2,1)S(1)}, u32[]{:S(2)}, u32[]{:S(2)}) collective-permute-start(bf16[2,2,256,256]{3,2,1,0:T(8,128)(2,1)} %get-tuple-element.15), channel_id=1, source_target_pairs={{0,16},{16,0},{1,17},{17,1},{2,18},{18,2},{3,19},{19,3},{4,20},{20... | collective-permute-start | bytes 1572872 | tf_op jit(solution)/shard_map/ppermute | solution.py:196
  59.7 0.8 %copy-start.3 = (bf16[2,2,256,256]{3,2,1,0:T(8,128)(2,1)}, bf16[2,2,256,256]{3,2,1,0:T(8,128)(2,1)S(1)}, u32[]{:S(2)}) copy-start(bf16[2,2,256,256]{3,2,1,0:T(8,128)(2,1)S(1)} %collective-permute-done.3.arrived) | copy-start | bytes 1572868
  64.8 11.5 %collective-permute-start.4 = (bf16[2,128,1024]{2,1,0:T(8,128)(2,1)}, bf16[2,128,1024]{2,1,0:T(8,128)(2,1)S(1)}, u32[]{:S(2)}, u32[]{:S(2)}) collective-permute-start(bf16[2,128,1024]{2,1,0:T(8,128)(2,1)} %get-tuple-element.17), channel_id=1, source_target_pairs={{0,1},{1,2},{2,3},{3,4},{4,5},{5,6},{6,7},{7,8},{8,9},{9,10},{10,1... | collective-permute-start | bytes 1572872 | tf_op jit(solution)/shard_map/ppermute | solution.py:206
  64.8 11.5 %collective-permute-start.5 = (bf16[2,128,1024]{2,1,0:T(8,128)(2,1)}, bf16[2,128,1024]{2,1,0:T(8,128)(2,1)S(1)}, u32[]{:S(2)}, u32[]{:S(2)}) collective-permute-start(bf16[2,128,1024]{2,1,0:T(8,128)(2,1)} %get-tuple-element.18), channel_id=1, source_target_pairs={{0,15},{1,0},{2,1},{3,2},{4,3},{5,4},{6,5},{7,6},{8,7},{9,8},{10,9... | collective-permute-start | bytes 1572872 | tf_op jit(solution)/shard_map/ppermute | solution.py:207

commit v2 on v1

v2 whole, which is shorter than its diff:
```python
import functools
import jax
import jax.numpy as jnp
import numpy as np
from jax import lax
from jax.experimental import pallas as pl
from jax.experimental.pallas import tpu as pltpu
from jax.sharding import PartitionSpec as P

modulus_floor = 0.25
LANES = 128
SUBLANES = 8
VMEM = pl.BlockSpec(memory_space=pltpu.VMEM)
SMEM = pl.BlockSpec(memory_space=pltpu.SMEM)
LIMIT = pltpu.CompilerParams(vmem_limit_bytes=60000 * 1024)


def dft_blocks(side):
    indices = np.arange(side)
    angles = (indices[:, None] * indices[None, :] % side) * (2.0 * np.pi / side)
    real = np.cos(angles) / np.sqrt(side)
    imag = np.sin(angles) / np.sqrt(side)
    tables = []
    for sign in (-1.0, 1.0):
        tables.append(np.block([[real, -sign * imag], [sign * imag, real]]))
        tables.append(np.block([[real, sign * imag], [-sign * imag, real]]))
    return jnp.asarray(np.stack(tables), dtype=jnp.bfloat16)


def split_col(col, cols, side):
    base = jnp.minimum(lax.div(col, LANES), (cols - side) // LANES - 1) * LANES
    return base, col - base


def cut_window(ext, plane, row, col, height, side):
    base, shift = split_col(col, ext.shape[2], side)
    top = lax.div(row, SUBLANES) * SUBLANES
    tall = height + SUBLANES
    block = ext[plane, pl.ds(top, tall), pl.ds(base, side + LANES)]
    block = pltpu.roll(block, lax.rem(tall + top - row, tall), axis=0)[:height]
    back = lax.rem(LANES - shift + LANES, LANES)
    chunks = [
        pltpu.roll(block[:, j : j + LANES], back, axis=1) for j in range(0, side + LANES, LANES)
    ]
    lane = lax.broadcasted_iota(jnp.int32, (height, LANES), 1)
    keep = lane < LANES - shift
    return jnp.concatenate(
        [jnp.where(keep, chunks[j], chunks[j + 1]) for j in range(len(chunks) - 1)], axis=1
    )


def add_window(grad, plane, row, col, field):
    height, side = field.shape
    base, shift = split_col(col, grad.shape[2], side)
    top = lax.div(row, SUBLANES) * SUBLANES
    tall = height + SUBLANES
    field = jnp.concatenate([field, jnp.zeros((SUBLANES, side), field.dtype)], axis=0)
    field = pltpu.roll(field, row - top, axis=0)
    ahead = lax.rem(shift, LANES)
    chunks = [pltpu.roll(field[:, j : j + LANES], ahead, axis=1) for j in range(0, side, LANES)]
    lane = lax.broadcasted_iota(jnp.int32, (tall, LANES), 1)
    keep = lane >= shift
    zero = jnp.zeros((tall, LANES), field.dtype)
    parts = [zero] + chunks + [zero]
    placed = jnp.concatenate(
        [jnp.where(keep, parts[j + 1], parts[j]) for j in range(len(chunks) + 1)], axis=1
    )
    where = (plane, pl.ds(top, tall), pl.ds(base, side + LANES))
    grad[where] = grad[where] + placed


def dot(left, right):
    return jnp.dot(left, right, preferred_element_type=jnp.float32)


def transform(field, tables, which):
    side = field[0].shape[0]
    stacked = jnp.concatenate([field[0].astype(jnp.bfloat16), field[1].astype(jnp.bfloat16)], axis=0)
    middle = dot(tables[which], stacked).astype(jnp.bfloat16)
    beside = jnp.concatenate([middle[:side], middle[side:]], axis=1)
    result = dot(beside, tables[which + 1])
    return result[:, :side], result[:, side:]


def multiply(left, right):
    return left[0] * right[0] - left[1] * right[1], left[0] * right[1] + left[1] * right[0]


def multiply_conjugate(left, right):
    return left[0] * right[0] + left[1] * right[1], left[0] * right[1] - left[1] * right[0]


def narrowed(field):
    return tuple(part.astype(jnp.bfloat16).astype(jnp.float32) for part in field)


def one_position(psi0, object0, object1, measured, wave, tables):
    psi1 = narrowed(
        transform(multiply(wave, transform(multiply(psi0, object0), tables, 0)), tables, 2)
    )
    far = transform(multiply(psi1, object1), tables, 0)
    modulus = jnp.sqrt(far[0] * far[0] + far[1] * far[1])
    factor = 1.0 - measured / jnp.maximum(modulus, modulus_floor)
    g1 = narrowed(transform((far[0] * factor, far[1] * factor), tables, 2))
    d1 = multiply_conjugate(psi1, g1)
    back = transform(multiply_conjugate(object1, g1), tables, 0)
    g0 = narrowed(transform(multiply_conjugate(wave, back), tables, 2))
    return multiply_conjugate(psi0, g0), d1


def wide(ref, *index):
    return ref[index + (0,)].astype(jnp.float32), ref[index + (1,)].astype(jnp.float32)


def pick(info, kind, side_index, rank, values):
    seen = jnp.int32(0)
    chosen = jnp.int32(0)
    for position in range(info.shape[1]):
        above = info[0, position] < 0
        here = above if side_index == 0 else jnp.logical_not(above)
        match = jnp.logical_and(here, seen == rank)
        chosen = chosen + jnp.where(match, values(position), 0)
        seen = seen + jnp.where(here, 1, 0)
    return chosen


def corner(info, side_index, rank):
    row = pick(info, 0, side_index, rank, lambda position: info[0, position])
    col = pick(info, 1, side_index, rank, lambda position: info[1, position])
    return row, col


def near_rows(side_index, side):
    return (side // 4, side) if side_index == 0 else (0, side - side // 4)


def far_rows(side_index, side):
    return (0, side // 2) if side_index == 0 else (side // 2, side)


def wave_kernel(
    side, count, here, before, after, choice,
    band, probes_any, amps_any, wave_any, tables_any,
    mine, near_out, far_out,
    ext, probes, amps, wave, tables,
    near_send, far_send, near_in, far_in, near_back, far_back,
    local_sem, send_sem, recv_sem,
):
    rim = side // 2
    quarter = side // 4
    band_rows = band.shape[1]
    c = lax.axis_index("cuts")
    region = lax.axis_index("region")
    other_cut = 1 - c
    prior = lax.rem(region + count - 1, count)
    following = lax.rem(region + 1, count)
    loads = [
        pltpu.make_async_copy(source, target, local_sem.at[k])
        for k, (source, target) in enumerate((
            (band, ext.at[:, pl.ds(rim, band_rows)]),
            (probes_any, probes), (amps_any, amps), (wave_any, wave), (tables_any, tables),
        ))
    ]
    for load in loads:
        load.start()
    barrier = pltpu.get_barrier_semaphore()
    peers = [(other_cut, region)]
    peers += [(q, t) for q in (c, other_cut) for t in (prior, following)]
    for peer in peers:
        pl.semaphore_signal(barrier, 1, device_id=peer, device_id_type=pl.DeviceIdType.MESH)
    loads[0].wait()

    def remote(source, target, slot, peer):
        return pltpu.make_async_remote_copy(
            src_ref=source, dst_ref=target,
            send_sem=send_sem.at[slot], recv_sem=recv_sem.at[slot],
            device_id=peer, device_id_type=pl.DeviceIdType.MESH,
        )

    sends = [[], []]
    for d in range(2):
        row, col = corner(here, d, other_cut)
        low, high = near_rows(d, side)
        for plane in range(2):
            near_send[d, plane] = cut_window(
                ext, plane, row + rim + low, col, high - low, side
            ).astype(jnp.bfloat16)
        sends[d].append(remote(near_send.at[d], near_in.at[d], 6 * d, (other_cut, region)))
        if d == 0:
            pl.semaphore_wait(barrier, len(peers))
        sends[d][0].start()
        info, peer_region, offset = (
            (after, following, band_rows) if d == 0 else (before, prior, -band_rows)
        )
        low, high = far_rows(d, side)
        for j, q in enumerate((c, other_cut)):
            row, col = corner(info, d, q)
            for plane in range(2):
                far_send[d, j, plane] = cut_window(
                    ext, plane, row + rim + offset + low, col, high - low, side
                ).astype(jnp.bfloat16)
            copy = remote(far_send.at[d, j], far_in.at[d, j], 6 * d + 1 + j, (q, peer_region))
            copy.start()
            sends[d].append(copy)
    for load in loads[1:]:
        load.wait()
    first = c == 0
    backs = []
    ids = lax.broadcasted_iota(jnp.int32, (rim, side), 0)
    for d in range(2):
        position = pick(here, 0, d, c, lambda p: p)
        chosen = pick(here, 0, d, c, lambda p: choice[p])
        row, col = corner(here, d, c)
        psi0 = wide(probes, chosen)
        own = [cut_window(ext, plane, row + rim, col, side, side) for plane in range(2)]
        for copy in sends[d]:
            copy.wait_recv()
        other = []
        for plane in range(2):
            far = far_in[d, 0, plane].astype(jnp.float32)
            far_other = far_in[d, 1, plane].astype(jnp.float32)
            near_other = near_in[d, plane].astype(jnp.float32)
            near_own = own[plane]
            if d == 0:
                mixed = jnp.where(ids < -row, far, near_own[:rim])
                own[plane] = jnp.concatenate([mixed, near_own[rim:]], axis=0)
                mixed = jnp.where(ids[quarter:] < -row, far_other[quarter:], near_other[:quarter])
                parts = [far_other[:quarter], mixed, near_other[quarter:]]
            else:
                mixed = jnp.where(ids >= rim - row, far, near_own[rim:])
                own[plane] = jnp.concatenate([near_own[:rim], mixed], axis=0)
                mixed = jnp.where(ids[:quarter] >= rim - row, far_other[:quarter], near_other[rim:])
                parts = [near_other[:rim], mixed, far_other[quarter:]]
            other.append(jnp.concatenate(parts, axis=0))
        object0 = tuple(jnp.where(first, x, y) for x, y in zip(own, other))
        object1 = tuple(jnp.where(first, y, x) for x, y in zip(own, other))
        d0, d1 = one_position(psi0, object0, object1, amps[position], (wave[0], wave[1]), tables)
        peer_region = prior if d == 0 else following
        near_low, near_high = near_rows(d, side)
        low, high = far_rows(d, side)
        for plane in range(2):
            kept = jnp.where(first, d0[plane], d1[plane]).astype(jnp.bfloat16)
            given = jnp.where(first, d1[plane], d0[plane]).astype(jnp.bfloat16)
            mine[d, plane] = kept[near_low:near_high]
            near_back[d, plane] = given[near_low:near_high]
            far_back[d, 0, plane] = kept[low:high]
            far_back[d, 1, plane] = given[low:high]
        backs.append(remote(near_back.at[d], near_out.at[d], 6 * d + 3, (other_cut, region)))
        for j, q in enumerate((c, other_cut)):
            backs.append(
                remote(far_back.at[d, j], far_out.at[d, j], 6 * d + 4 + j, (q, peer_region))
            )
        for copy in backs[-3:]:
            copy.start()
    for copy in sends[0] + sends[1]:
        copy.wait_send()
    for copy in backs:
        copy.wait()


def deposit_kernel(side, here, before, after, cut, mine, near, far, out, grad):
    rim = side // 2
    band_rows = out.shape[1]
    c = cut[0]
    grad[...] = jnp.zeros_like(grad)
    for d in range(2):
        low, _ = near_rows(d, side)
        far_low, _ = far_rows(d, side)
        info, offset = (after, band_rows) if d == 0 else (before, -band_rows)
        parts = [
            (mine.at[d], here, c, rim + low),
            (near.at[d], here, 1 - c, rim + low),
            (far.at[d, 0], info, c, rim + offset + far_low),
            (far.at[d, 1], info, 1 - c, rim + offset + far_low),
        ]
        for source, table, rank, shift in parts:
            row, col = corner(table, d, rank)
            for plane in range(2):
                add_window(grad, plane, row + shift, col, source[plane].astype(jnp.float32))
    out[...] = grad[:, rim : rim + band_rows]


def shards(objects, probes, amplitudes, prop_phase, scan_rows, scan_cols, probe_choice):
    side = probes.shape[-1]
    rim = side // 2
    count = lax.axis_size("region")
    band = objects[0]
    band_rows, columns = band.shape[1:]
    cut = lax.axis_index("cuts").astype(jnp.int32)[None]
    here = jnp.stack([scan_rows, scan_cols])
    before = lax.ppermute(here, "region", [(i, (i + 1) % count) for i in range(count)])
    after = lax.ppermute(here, "region", [(i, (i - 1) % count) for i in range(count)])
    wave = jnp.stack([jnp.cos(prop_phase), jnp.sin(prop_phase)])
    tables = dft_blocks(side)
    near = (2, 2, side - side // 4, side)
    far = (2, 2, 2, rim, side)
    held = lambda shape: jax.ShapeDtypeStruct(shape, jnp.bfloat16)
    slot = lambda shape: pltpu.VMEM(shape, jnp.bfloat16)
    tall = pltpu.VMEM((2, band_rows + 2 * rim + SUBLANES, columns), jnp.float32)
    ANY = pl.BlockSpec(memory_space=pl.ANY)
    mine, near_part, far_part = pl.pallas_call(
        functools.partial(wave_kernel, side, count),
        out_shape=(held(near), held(near), held(far)),
        in_specs=[SMEM] * 4 + [ANY] * 5,
        out_specs=(VMEM, VMEM, VMEM),
        scratch_shapes=[
            tall,
            pltpu.VMEM(probes.shape, probes.dtype),
            pltpu.VMEM(amplitudes.shape, amplitudes.dtype),
            pltpu.VMEM(wave.shape, wave.dtype),
            pltpu.VMEM(tables.shape, tables.dtype),
            slot(near), slot(far), slot(near), slot(far), slot(near), slot(far),
            pltpu.SemaphoreType.DMA((5,)),
            pltpu.SemaphoreType.DMA((12,)),
            pltpu.SemaphoreType.DMA((12,)),
        ],
        compiler_params=pltpu.CompilerParams(
            collective_id=0, has_side_effects=True, vmem_limit_bytes=60000 * 1024
        ),
    )(here, before, after, probe_choice, band, probes, amplitudes, wave, tables)
    out = pl.pallas_call(
        functools.partial(deposit_kernel, side),
        out_shape=jax.ShapeDtypeStruct(band.shape, jnp.float32),
        in_specs=[SMEM] * 4 + [VMEM] * 3,
        out_specs=VMEM,
        scratch_shapes=[tall],
        compiler_params=LIMIT,
    )(here, before, after, cut, mine, near_part, far_part)
    return out[None]


def solution(mesh):
    return jax.shard_map(
        shards,
        mesh=mesh,
        in_specs=(
            P("cuts", None, "region", None),
            P(),
            P("region", None, None),
            P(),
            P("region"),
            P("region"),
            P("region"),
        ),
        out_specs=P("cuts", None, "region", None),
        check_vma=False,
    )
```

time: 79.9 us -> 49.5 us (0.62)
  waiting for transfers between devices: 37.1 us -> 3 us
  Pallas kernels: 20.2 us -> 36.3 us
  starting transfers between devices: 13 us -> 5.53 us
  other arithmetic: 5.98 us -> 1.51 us
  local copies, waits for them, and re-layouts: 3.41 us -> 2.43 us
    ppermute x6 -> x2, waiting for transfers between devices: 37.1 us -> 3 us  [the longest x1 3 us: shards(): lax.ppermute(here, 'region', [(i, (i + 1) % count) for i in range(count)])]
    pallas_call x3 -> x2, Pallas kernels: 20.2 us -> 36.3 us  [the longest x1 32 us: shards(): pl.pallas_call(functools.partial(wave_kernel, side, count), out_shape=(he...]
    ppermute x6 -> x2, starting transfers between devices: 13 us -> 5.53 us  [the longest x1 5.53 us: shards(): lax.ppermute(here, 'region', [(i, (i - 1) % count) for i in range(count)])]
    broadcast_in_dim x1 -> x0, other arithmetic: 3.37 us -> none  [shards(): return (inner + rims)[None]]
    unnamed x10 -> x6, local copies, waits for them, and re-layouts: 2.39 us -> 0.57 us
    another operation x1, other arithmetic: 1.74 us -> 0.68 us  [shards(): here = jnp.stack([scan_rows, scan_cols])]
    another operation x1, local copies, waits for them, and re-layouts: 0.95 us -> 1.85 us  [shards(): wave = jnp.stack([jnp.cos(prop_phase), jnp.sin(prop_phase)])]
  transfers between devices with their start and end apart: 6 -> 2, of which waited for: 5 -> 1; matrix products, arithmetic and copies ran while one was open for 2% -> 5% of each run, Pallas kernels for 0% -> 0%
where the time goes in v2:
time: 49.5 us; the launch traced here: 48.8 us
  Pallas kernels  36.3 us (73%)
  starting transfers between devices  5.53 us (11%)
  waiting for transfers between devices  3 us (6%)
  local copies, waits for them, and re-layouts  2.43 us (5%)
  other arithmetic  1.51 us (3%)
    pallas_call x1, Pallas kernels, shards(): pl.pallas_call(functools.partial(wave_kernel, side, count), out_shape=(he...  32 us
    ppermute x1, starting transfers between devices, shards(): lax.ppermute(here, 'region', [(i, (i - 1) % count) for i in range(count)])  5.53 us
    pallas_call x1, Pallas kernels, shards(): pl.pallas_call(functools.partial(deposit_kernel, side), out_shape=jax.Sha...  4.26 us
    ppermute x1, waiting for transfers between devices, shards(): lax.ppermute(here, 'region', [(i, (i + 1) % count) for i in range(count)])  3 us
    another operation x1, local copies, waits for them, and re-layouts, shards(): wave = jnp.stack([jnp.cos(prop_phase), jnp.sin(prop_phase)])  1.85 us
  transfers between devices with their start and end apart: 2, of which 1 were waited for; matrix products, arithmetic and copies ran while one was open for 5% of the time, Pallas kernels for 0%

profile of v2, /device:TPU:0, one launch (start us, length us, event | category | flops | bytes accessed | tf_op | source)
XLA Modules:
  0.0 48.8 jit_solution(1759130251860623458)
XLA Ops:
  0.0 0.7 %pad_add_fusion.here = s32[2,4]{1,0:T(2,128)S(1)} fusion(s32[1,4]{1,0:T(1,128)} %bitcast.10, s32[1,4]{1,0:T(1,128)} %bitcast.11), kind=kLoop, calls=%fused_computation.3 | loop fusion | flops 8 | bytes 64 | tf_op jit(solution)/shard_map/stack | solution.py:290
  0.7 0.0 copy-start
  0.7 5.5 %collective-permute-start.1 = (s32[2,4]{1,0:T(2,128)S(1)}, s32[2,4]{1,0:T(2,128)S(1)}, u32[]{:S(2)}, u32[]{:S(2)}) collective-permute-start(s32[2,4]{1,0:T(2,128)S(1)} %pad_add_fusion.here), channel_id=1, source_target_pairs={{0,15},{1,0},{2,1},{3,2},{4,3},{5,4},{6,5},{7,6},{8,7},{9,8},{10,9... | collective-permute-start | bytes 104 | tf_op jit(solution)/shard_map/ppermute | solution.py:292
  6.2 0.0 collective-permute-start
  6.2 1.9 %cosine_bitcast_fusion = (f32[1,256,256]{2,1,0:T(8,128)S(1)}, f32[1,256,256]{2,1,0:T(8,128)S(1)}) fusion(f32[256,256]{1,0:T(8,128)} %param.11), kind=kLoop, calls=%fused_computation.2 | loop fusion | bytes 786432 | tf_op jit(solution)/shard_map/stack | solution.py:293
  8.1 0.8 %pad_maximum_fusion.wave_any = f32[2,256,256]{2,1,0:T(8,128)} fusion(f32[1,256,256]{2,1,0:T(8,128)S(1)} %get-tuple-element.12, f32[1,256,256]{2,1,0:T(8,128)S(1)} %get-tuple-element.11), kind=kLoop, calls=%fused_computation | loop fusion | flops 131072 | bytes 1048576 | tf_op jit(solution)/shard_map/stack | solution.py:293
  8.9 0.0 collective-permute-done.1.after
  8.9 0.0 copy-start.1
  8.9 3.0 %collective-permute-done.before = s32[2,4]{1,0:T(2,128)S(1)} collective-permute-done((s32[2,4]{1,0:T(2,128)S(1)}, s32[2,4]{1,0:T(2,128)S(1)}, u32[]{:S(2)}, u32[]{:S(2)}) %collective-permute-start) | collective-permute-done | bytes 64 | tf_op jit(solution)/shard_map/ppermute | solution.py:291
  11.9 0.0 copy-start.2
  11.9 0.0 copy-done
  11.9 0.0 copy-done.1
  11.9 0.6 %copy-done.2 = s32[2,4]{1,0:T(2,128)} copy-done((s32[2,4]{1,0:T(2,128)}, s32[2,4]{1,0:T(2,128)S(1)}, u32[]{:S(2)}) %copy-start.2) | copy-done | bytes 56
  12.5 32.0 %shard_map.82 = (bf16[2,2,192,256]{3,2,1,0:T(8,128)(2,1)}, bf16[2,2,192,256]{3,2,1,0:T(8,128)(2,1)}, bf16[2,2,2,128,256]{4,3,2,1,0:T(8,128)(2,1)}) custom-call(s32[2,4]{1,0:T(2,128)} %copy-done, s32[2,4]{1,0:T(2,128)} %copy-done.2, s32[2,4]{1,0:T(2,128)} %copy-done.1, s32[4]{0:T(128)} %choice.1, f32[2,256,1024]{2,1,0:T(8,128)} %bitcast.9, ...), custom_call_target="tpu_custom_call" | custom-call | tf_op jit(solution)/shard_map/pallas_call | solution.py:301
  44.5 4.3 %shard_map.83 = f32[2,256,1024]{2,1,0:T(8,128)} custom-call(s32[2,4]{1,0:T(2,128)} %copy-done, s32[2,4]{1,0:T(2,128)} %copy-done.2, s32[2,4]{1,0:T(2,128)} %copy-done.1, s32[1]{0:T(128)} %bitcast.2.cut, bf16[2,2,192,256]{3,2,1,0:T(8,128)(2,1)} %get-tuple-element.8.mine, bf16[2,2,192,256]{3,2,1,0:T(8,128)(2,1)} %get-tuple-element.9.near, ...), custom_call_target="tpu_custom_call" | custom-call | tf_op jit(solution)/shard_map/pallas_call | solution.py:321
Async XLA Ops:
  0.7 11.2 %copy-start = (s32[2,4]{1,0:T(2,128)}, s32[2,4]{1,0:T(2,128)S(1)}, u32[]{:S(2)}) copy-start(s32[2,4]{1,0:T(2,128)S(1)} %pad_add_fusion.here) | copy-start | bytes 100
  0.7 8.2 %collective-permute-start.1 = (s32[2,4]{1,0:T(2,128)S(1)}, s32[2,4]{1,0:T(2,128)S(1)}, u32[]{:S(2)}, u32[]{:S(2)}) collective-permute-start(s32[2,4]{1,0:T(2,128)S(1)} %pad_add_fusion.here), channel_id=1, source_target_pairs={{0,15},{1,0},{2,1},{3,2},{4,3},{5,4},{6,5},{7,6},{8,7},{9,8},{10,9... | collective-permute-start | bytes 104 | tf_op jit(solution)/shard_map/ppermute | solution.py:292
  6.2 5.7 %collective-permute-start = (s32[2,4]{1,0:T(2,128)S(1)}, s32[2,4]{1,0:T(2,128)S(1)}, u32[]{:S(2)}, u32[]{:S(2)}) collective-permute-start(s32[2,4]{1,0:T(2,128)S(1)} %pad_add_fusion.here), channel_id=1, source_target_pairs={{0,1},{1,2},{2,3},{3,4},{4,5},{5,6},{6,7},{7,8},{8,9},{9,10},{10,1... | collective-permute-start | bytes 104 | tf_op jit(solution)/shard_map/ppermute | solution.py:291
  8.9 3.0 %copy-start.1 = (s32[2,4]{1,0:T(2,128)}, s32[2,4]{1,0:T(2,128)S(1)}, u32[]{:S(2)}) copy-start(s32[2,4]{1,0:T(2,128)S(1)} %collective-permute-done.1.after) | copy-start | bytes 100
  11.9 0.6 %copy-start.2 = (s32[2,4]{1,0:T(2,128)}, s32[2,4]{1,0:T(2,128)S(1)}, u32[]{:S(2)}) copy-start(s32[2,4]{1,0:T(2,128)S(1)} %collective-permute-done.before) | copy-start | bytes 100

commit v3 on v2

--- a/solution.py
+++ b/solution.py
@@ -115,8 +115,8 @@
 def pick(info, kind, side_index, rank, values):
     seen = jnp.int32(0)
     chosen = jnp.int32(0)
-    for position in range(info.shape[1]):
-        above = info[0, position] < 0
+    for position in range(info[0].shape[0]):
+        above = info[0][position] < 0
         here = above if side_index == 0 else jnp.logical_not(above)
         match = jnp.logical_and(here, seen == rank)
         chosen = chosen + jnp.where(match, values(position), 0)
@@ -125,8 +125,8 @@
 
 
 def corner(info, side_index, rank):
-    row = pick(info, 0, side_index, rank, lambda position: info[0, position])
-    col = pick(info, 1, side_index, rank, lambda position: info[1, position])
+    row = pick(info, 0, side_index, rank, lambda position: info[0][position])
+    col = pick(info, 1, side_index, rank, lambda position: info[1][position])
     return row, col
 
 
@@ -139,12 +139,11 @@
 
 
 def wave_kernel(
-    side, count, here, before, after, choice,
-    band, probes_any, amps_any, wave_any, tables_any,
-    mine, near_out, far_out,
-    ext, probes, amps, wave, tables,
-    near_send, far_send, near_in, far_in, near_back, far_back,
-    local_sem, send_sem, recv_sem,
+    side, count, scans, choice_any, band, probes_any, amps_any, phase_any, tables_any,
+    mine, near_out, far_out, around,
+    ext, probes, amps, phase, wave, tables,
+    near_send, far_send, near_in, far_in, near_back, far_back, here, before, after, choice,
+    local_sem, info_sem, send_sem, recv_sem,
 ):
     rim = side // 2
     quarter = side // 4
@@ -157,8 +156,9 @@
     loads = [
         pltpu.make_async_copy(source, target, local_sem.at[k])
         for k, (source, target) in enumerate((
-            (band, ext.at[:, pl.ds(rim, band_rows)]),
-            (probes_any, probes), (amps_any, amps), (wave_any, wave), (tables_any, tables),
+            (scans[0], here[0]), (scans[1], here[1]), (choice_any, choice),
+            (band, ext.at[:, pl.ds(rim, band_rows)]), (phase_any, phase),
+            (tables_any, tables), (probes_any, probes), (amps_any, amps),
         ))
     ]
     for load in loads:
@@ -168,7 +168,7 @@
     peers += [(q, t) for q in (c, other_cut) for t in (prior, following)]
     for peer in peers:
         pl.semaphore_signal(barrier, 1, device_id=peer, device_id_type=pl.DeviceIdType.MESH)
-    loads[0].wait()
+    pl.semaphore_wait(barrier, len(peers))
 
     def remote(source, target, slot, peer):
         return pltpu.make_async_remote_copy(
@@ -177,6 +177,12 @@
             device_id=peer, device_id_type=pl.DeviceIdType.MESH,
         )
 
+    notes = []
+    for k, (source, target) in enumerate(zip(scans + scans, around)):
+        notes.append(remote(source, target, 12 + k, (c, following if k < 2 else prior)))
+        notes[-1].start()
+    for load in loads[:4]:
+        load.wait()
     sends = [[], []]
     for d in range(2):
         row, col = corner(here, d, other_cut)
@@ -186,9 +192,15 @@
                 ext, plane, row + rim + low, col, high - low, side
             ).astype(jnp.bfloat16)
         sends[d].append(remote(near_send.at[d], near_in.at[d], 6 * d, (other_cut, region)))
+        sends[d][0].start()
         if d == 0:
-            pl.semaphore_wait(barrier, len(peers))
-        sends[d][0].start()
+            fetches = []
+            for k, target in enumerate(before + after):
+                notes[k].wait()
+                fetches.append(pltpu.make_async_copy(around[k], target, info_sem.at[k]))
+                fetches[-1].start()
+            for fetch in fetches:
+                fetch.wait()
         info, peer_region, offset = (
             (after, following, band_rows) if d == 0 else (before, prior, -band_rows)
         )
@@ -202,8 +214,10 @@
             copy = remote(far_send.at[d, j], far_in.at[d, j], 6 * d + 1 + j, (q, peer_region))
             copy.start()
             sends[d].append(copy)
-    for load in loads[1:]:
+    for load in loads[4:]:
         load.wait()
+    wave[0] = jnp.cos(phase[...])
+    wave[1] = jnp.sin(phase[...])
     first = c == 0
     backs = []
     ids = lax.broadcasted_iota(jnp.int32, (rim, side), 0)
@@ -258,26 +272,44 @@
         copy.wait()
 
 
-def deposit_kernel(side, here, before, after, cut, mine, near, far, out, grad):
+def deposit_kernel(
+    side, scans, around, mine, near, far, out, grad, here, before, after, local_sem, out_sem
+):
     rim = side // 2
     band_rows = out.shape[1]
-    c = cut[0]
+    c = lax.axis_index("cuts")
+    loads = [
+        pltpu.make_async_copy(source, target, local_sem.at[k])
+        for k, (source, target) in enumerate(zip(scans + around, here + before + after))
+    ]
+    for load in loads:
+        load.start()
     grad[...] = jnp.zeros_like(grad)
-    for d in range(2):
-        low, _ = near_rows(d, side)
-        far_low, _ = far_rows(d, side)
-        info, offset = (after, band_rows) if d == 0 else (before, -band_rows)
-        parts = [
-            (mine.at[d], here, c, rim + low),
-            (near.at[d], here, 1 - c, rim + low),
-            (far.at[d, 0], info, c, rim + offset + far_low),
-            (far.at[d, 1], info, 1 - c, rim + offset + far_low),
-        ]
-        for source, table, rank, shift in parts:
-            row, col = corner(table, d, rank)
-            for plane in range(2):
+    for load in loads:
+        load.wait()
+    stores = []
+    for plane in range(2):
+        for d in range(2):
+            low, _ = near_rows(d, side)
+            far_low, _ = far_rows(d, side)
+            info, offset = (after, band_rows) if d == 0 else (before, -band_rows)
+            parts = [
+                (mine.at[d], here, c, rim + low),
+                (near.at[d], here, 1 - c, rim + low),
+                (far.at[d, 0], info, c, rim + offset + far_low),
+                (far.at[d, 1], info, 1 - c, rim + offset + far_low),
+            ]
+            for source, table, rank, shift in parts:
+                row, col = corner(table, d, rank)
                 add_window(grad, plane, row + shift, col, source[plane].astype(jnp.float32))
-    out[...] = grad[:, rim : rim + band_rows]
+        stores.append(
+            pltpu.make_async_copy(
+                grad.at[plane, pl.ds(rim, band_rows)], out.at[plane], out_sem.at[plane]
+            )
+        )
+        stores[-1].start()
+    for store in stores:
+        store.wait()
 
 
 def shards(objects, probes, amplitudes, prop_phase, scan_rows, scan_cols, probe_choice):
@@ -286,11 +318,6 @@
     count = lax.axis_size("region")
     band = objects[0]
     band_rows, columns = band.shape[1:]
-    cut = lax.axis_index("cuts").astype(jnp.int32)[None]
-    here = jnp.stack([scan_rows, scan_cols])
-    before = lax.ppermute(here, "region", [(i, (i + 1) % count) for i in range(count)])
-    after = lax.ppermute(here, "region", [(i, (i - 1) % count) for i in range(count)])
-    wave = jnp.stack([jnp.cos(prop_phase), jnp.sin(prop_phase)])
     tables = dft_blocks(side)
     near = (2, 2, side - side // 4, side)
     far = (2, 2, 2, rim, side)
@@ -298,34 +325,44 @@
     slot = lambda shape: pltpu.VMEM(shape, jnp.bfloat16)
     tall = pltpu.VMEM((2, band_rows + 2 * rim + SUBLANES, columns), jnp.float32)
     ANY = pl.BlockSpec(memory_space=pl.ANY)
-    mine, near_part, far_part = pl.pallas_call(
+    scans = (scan_rows, scan_cols)
+    info = jax.ShapeDtypeStruct(scan_rows.shape, jnp.int32)
+    scalars = pltpu.SMEM(scan_rows.shape, jnp.int32)
+    mine, near_part, far_part, around = pl.pallas_call(
         functools.partial(wave_kernel, side, count),
-        out_shape=(held(near), held(near), held(far)),
-        in_specs=[SMEM] * 4 + [ANY] * 5,
-        out_specs=(VMEM, VMEM, VMEM),
+        out_shape=(held(near), held(near), held(far), (info,) * 4),
+        in_specs=[(ANY, ANY)] + [ANY] * 6,
+        out_specs=(VMEM, VMEM, VMEM, (ANY,) * 4),
         scratch_shapes=[
             tall,
             pltpu.VMEM(probes.shape, probes.dtype),
             pltpu.VMEM(amplitudes.shape, amplitudes.dtype),
-            pltpu.VMEM(wave.shape, wave.dtype),
+            pltpu.VMEM(prop_phase.shape, jnp.float32),
+            pltpu.VMEM((2,) + prop_phase.shape, jnp.float32),
             pltpu.VMEM(tables.shape, tables.dtype),
             slot(near), slot(far), slot(near), slot(far), slot(near), slot(far),
-            pltpu.SemaphoreType.DMA((5,)),
-            pltpu.SemaphoreType.DMA((12,)),
-            pltpu.SemaphoreType.DMA((12,)),
+            (scalars,) * 2, (scalars,) * 2, (scalars,) * 2, scalars,
+            pltpu.SemaphoreType.DMA((8,)),
+            pltpu.SemaphoreType.DMA((4,)),
+            pltpu.SemaphoreType.DMA((16,)),
+            pltpu.SemaphoreType.DMA((16,)),
         ],
         compiler_params=pltpu.CompilerParams(
             collective_id=0, has_side_effects=True, vmem_limit_bytes=60000 * 1024
         ),
-    )(here, before, after, probe_choice, band, probes, amplitudes, wave, tables)
+    )(scans, probe_choice, band, probes, amplitudes, prop_phase, tables)
     out = pl.pallas_call(
         functools.partial(deposit_kernel, side),
         out_shape=jax.ShapeDtypeStruct(band.shape, jnp.float32),
-        in_specs=[SMEM] * 4 + [VMEM] * 3,
-        out_specs=VMEM,
-        scratch_shapes=[tall],
+        in_specs=[(ANY, ANY), (ANY,) * 4] + [VMEM] * 3,
+        out_specs=ANY,
+        scratch_shapes=[
+            tall, (scalars,) * 2, (scalars,) * 2, (scalars,) * 2,
+            pltpu.SemaphoreType.DMA((6,)),
+            pltpu.SemaphoreType.DMA((2,)),
+        ],
         compiler_params=LIMIT,
-    )(here, before, after, cut, mine, near_part, far_part)
+    )(scans, around, mine, near_part, far_part)
     return out[None]
 
 

time: 49.5 us -> 41.3 us (0.83)
  the two profiles are of different devices: /device:TPU:0 before, /device:TPU:1 now
where the time goes in v3:
time: 41.3 us; the launch traced here: 41.1 us
  Pallas kernels  41.1 us (100%)
    pallas_call x1, Pallas kernels, shards(): pl.pallas_call(functools.partial(wave_kernel, side, count), out_shape=(he...  36.8 us
    pallas_call x1, Pallas kernels, shards(): pl.pallas_call(functools.partial(deposit_kernel, side), out_shape=jax.Sha...  4.33 us

profile of v3, /device:TPU:1, one launch (start us, length us, event | category | flops | bytes accessed | tf_op | source)
XLA Modules:
  0.0 41.1 jit_solution(11491069013671849660)
XLA Ops:
  0.0 36.8 %shard_map.82 = (bf16[2,2,192,256]{3,2,1,0:T(8,128)(2,1)}, bf16[2,2,192,256]{3,2,1,0:T(8,128)(2,1)}, bf16[2,2,2,128,256]{4,3,2,1,0:T(8,128)(2,1)}, s32[4]{0:T(12...) custom-call(s32[4]{0:T(128)} %scans_0_.3, s32[4]{0:T(128)} %scans_1_.3, s32[4]{0:T(128)} %choice_any.1, ...), custom_call_target="tpu_custom_call" | custom-call | tf_op jit(solution)/shard_map/pallas_call | solution.py:331
  36.8 4.3 %shard_map.83 = f32[2,256,1024]{2,1,0:T(8,128)} custom-call(s32[4]{0:T(128)} %scans_0_.3, s32[4]{0:T(128)} %scans_1_.3, s32[4]{0:T(128)} %get-tuple-element.12.around_0_, s32[4]{0:T(128)} %get-tuple-element.13.around_1_, s32[4]{0:T(128)} %get-tuple-element.14.around_2_, s32[4]{0:T(128)} %get-tuple-element.15.around_3_, ...), custom_call_target="tpu_custom_call" | custom-call | tf_op jit(solution)/shard_map/pallas_call | solution.py:354

commit v4 on v3

--- a/solution.py
+++ b/solution.py
@@ -140,9 +140,9 @@
 
 def wave_kernel(
     side, count, scans, choice_any, band, probes_any, amps_any, phase_any, tables_any,
-    mine, near_out, far_out, around,
+    mine, full_out, near_out, far_out, around,
     ext, probes, amps, phase, wave, tables,
-    near_send, far_send, near_in, far_in, near_back, far_back, here, before, after, choice,
+    near_send, far_send, near_in, far_in, full_back, near_back, far_back, here, before, after, choice,
     local_sem, info_sem, send_sem, recv_sem,
 ):
     rim = side // 2
@@ -168,7 +168,6 @@
     peers += [(q, t) for q in (c, other_cut) for t in (prior, following)]
     for peer in peers:
         pl.semaphore_signal(barrier, 1, device_id=peer, device_id_type=pl.DeviceIdType.MESH)
-    pl.semaphore_wait(barrier, len(peers))
 
     def remote(source, target, slot, peer):
         return pltpu.make_async_remote_copy(
@@ -177,13 +176,8 @@
             device_id=peer, device_id_type=pl.DeviceIdType.MESH,
         )
 
-    notes = []
-    for k, (source, target) in enumerate(zip(scans + scans, around)):
-        notes.append(remote(source, target, 12 + k, (c, following if k < 2 else prior)))
-        notes[-1].start()
     for load in loads[:4]:
         load.wait()
-    sends = [[], []]
     for d in range(2):
         row, col = corner(here, d, other_cut)
         low, high = near_rows(d, side)
@@ -191,6 +185,13 @@
             near_send[d, plane] = cut_window(
                 ext, plane, row + rim + low, col, high - low, side
             ).astype(jnp.bfloat16)
+    pl.semaphore_wait(barrier, len(peers))
+    notes = []
+    for k, (source, target) in enumerate(zip(scans + scans, around)):
+        notes.append(remote(source, target, 12 + k, (c, following if k < 2 else prior)))
+        notes[-1].start()
+    sends = [[], []]
+    for d in range(2):
         sends[d].append(remote(near_send.at[d], near_in.at[d], 6 * d, (other_cut, region)))
         sends[d][0].start()
         if d == 0:
@@ -256,16 +257,29 @@
             kept = jnp.where(first, d0[plane], d1[plane]).astype(jnp.bfloat16)
             given = jnp.where(first, d1[plane], d0[plane]).astype(jnp.bfloat16)
             mine[d, plane] = kept[near_low:near_high]
-            near_back[d, plane] = given[near_low:near_high]
             far_back[d, 0, plane] = kept[low:high]
-            far_back[d, 1, plane] = given[low:high]
-        backs.append(remote(near_back.at[d], near_out.at[d], 6 * d + 3, (other_cut, region)))
-        for j, q in enumerate((c, other_cut)):
+            if d == 0:
+                full_back[plane] = given
+            else:
+                near_back[plane] = given[near_low:near_high]
+                far_back[d, 1, plane] = given[low:high]
+        if d == 0:
+            full = remote(full_back, full_out, 3, (other_cut, region))
+            full.start()
+        else:
             backs.append(
-                remote(far_back.at[d, j], far_out.at[d, j], 6 * d + 4 + j, (q, peer_region))
+                remote(far_back.at[d, 1], far_out.at[d, 1], 11, (other_cut, peer_region))
             )
-        for copy in backs[-3:]:
-            copy.start()
+            backs[-1].start()
+        backs.append(remote(far_back.at[d, 0], far_out.at[d, 0], 6 * d + 4, (c, peer_region)))
+        backs[-1].start()
+        if d == 1:
+            backs.append(remote(near_back, near_out, 9, (other_cut, region)))
+            backs[-1].start()
+    full.wait()
+    relay = remote(full_out.at[:, pl.ds(0, rim)], far_out.at[0, 1], 5, (c, prior))
+    relay.start()
+    backs.append(relay)
     for copy in sends[0] + sends[1]:
         copy.wait_send()
     for copy in backs:
@@ -273,7 +287,7 @@
 
 
 def deposit_kernel(
-    side, scans, around, mine, near, far, out, grad, here, before, after, local_sem, out_sem
+    side, scans, around, mine, full, near, far, out, grad, here, before, after, local_sem, out_sem
 ):
     rim = side // 2
     band_rows = out.shape[1]
@@ -295,7 +309,7 @@
             info, offset = (after, band_rows) if d == 0 else (before, -band_rows)
             parts = [
                 (mine.at[d], here, c, rim + low),
-                (near.at[d], here, 1 - c, rim + low),
+                (full.at[:, pl.ds(low, side - low)] if d == 0 else near, here, 1 - c, rim + low),
                 (far.at[d, 0], info, c, rim + offset + far_low),
                 (far.at[d, 1], info, 1 - c, rim + offset + far_low),
             ]
@@ -321,6 +335,7 @@
     tables = dft_blocks(side)
     near = (2, 2, side - side // 4, side)
     far = (2, 2, 2, rim, side)
+    full = (2, side, side)
     held = lambda shape: jax.ShapeDtypeStruct(shape, jnp.bfloat16)
     slot = lambda shape: pltpu.VMEM(shape, jnp.bfloat16)
     tall = pltpu.VMEM((2, band_rows + 2 * rim + SUBLANES, columns), jnp.float32)
@@ -328,11 +343,11 @@
     scans = (scan_rows, scan_cols)
     info = jax.ShapeDtypeStruct(scan_rows.shape, jnp.int32)
     scalars = pltpu.SMEM(scan_rows.shape, jnp.int32)
-    mine, near_part, far_part, around = pl.pallas_call(
+    mine, full_part, near_part, far_part, around = pl.pallas_call(
         functools.partial(wave_kernel, side, count),
-        out_shape=(held(near), held(near), held(far), (info,) * 4),
+        out_shape=(held(near), held(full), held(near[1:]), held(far), (info,) * 4),
         in_specs=[(ANY, ANY)] + [ANY] * 6,
-        out_specs=(VMEM, VMEM, VMEM, (ANY,) * 4),
+        out_specs=(VMEM, VMEM, VMEM, VMEM, (ANY,) * 4),
         scratch_shapes=[
             tall,
             pltpu.VMEM(probes.shape, probes.dtype),
@@ -340,7 +355,7 @@
             pltpu.VMEM(prop_phase.shape, jnp.float32),
             pltpu.VMEM((2,) + prop_phase.shape, jnp.float32),
             pltpu.VMEM(tables.shape, tables.dtype),
-            slot(near), slot(far), slot(near), slot(far), slot(near), slot(far),
+            slot(near), slot(far), slot(near), slot(far), slot(full), slot(near[1:]), slot(far),
             (scalars,) * 2, (scalars,) * 2, (scalars,) * 2, scalars,
             pltpu.SemaphoreType.DMA((8,)),
             pltpu.SemaphoreType.DMA((4,)),
@@ -354,7 +369,7 @@
     out = pl.pallas_call(
         functools.partial(deposit_kernel, side),
         out_shape=jax.ShapeDtypeStruct(band.shape, jnp.float32),
-        in_specs=[(ANY, ANY), (ANY,) * 4] + [VMEM] * 3,
+        in_specs=[(ANY, ANY), (ANY,) * 4] + [VMEM] * 4,
         out_specs=ANY,
         scratch_shapes=[
             tall, (scalars,) * 2, (scalars,) * 2, (scalars,) * 2,
@@ -362,7 +377,7 @@
             pltpu.SemaphoreType.DMA((2,)),
         ],
         compiler_params=LIMIT,
-    )(scans, around, mine, near_part, far_part)
+    )(scans, around, mine, full_part, near_part, far_part)
     return out[None]
 
 

time: 41.3 us -> 41.7 us (level)
  the two profiles are of different devices: /device:TPU:1 before, /device:TPU:0 now
where the time goes in v4:
time: 41.7 us; the launch traced here: 41.5 us
  Pallas kernels  41.5 us (100%)
    pallas_call x1, Pallas kernels, shards(): pl.pallas_call(functools.partial(wave_kernel, side, count), out_shape=(he...  37.2 us
    pallas_call x1, Pallas kernels, shards(): pl.pallas_call(functools.partial(deposit_kernel, side), out_shape=jax.Sha...  4.35 us

profile of v4, /device:TPU:0, one launch (start us, length us, event | category | flops | bytes accessed | tf_op | source)
XLA Modules:
  0.0 41.5 jit_solution(4028588576680347753)
XLA Ops:
  0.0 37.2 %shard_map.82 = (bf16[2,2,192,256]{3,2,1,0:T(8,128)(2,1)}, bf16[2,256,256]{2,1,0:T(8,128)(2,1)}, bf16[2,192,256]{2,1,0:T(8,128)(2,1)}, bf16[2,2,2,128,256]{4,3,2...) custom-call(s32[4]{0:T(128)} %scans_0_.3, s32[4]{0:T(128)} %scans_1_.3, s32[4]{0:T(128)} %choice_any.1, ...), custom_call_target="tpu_custom_call" | custom-call | tf_op jit(solution)/shard_map/pallas_call | solution.py:346
  37.2 4.3 %shard_map.83 = f32[2,256,1024]{2,1,0:T(8,128)} custom-call(s32[4]{0:T(128)} %scans_0_.3, s32[4]{0:T(128)} %scans_1_.3, s32[4]{0:T(128)} %get-tuple-element.13.around_0_, s32[4]{0:T(128)} %get-tuple-element.14.around_1_, s32[4]{0:T(128)} %get-tuple-element.15.around_2_, s32[4]{0:T(128)} %get-tuple-element.16.around_3_, ...), custom_call_target="tpu_custom_call" | custom-call | tf_op jit(solution)/shard_map/pallas_call | solution.py:369

commit v5 on v3

--- a/solution.py
+++ b/solution.py
@@ -168,7 +168,6 @@
     peers += [(q, t) for q in (c, other_cut) for t in (prior, following)]
     for peer in peers:
         pl.semaphore_signal(barrier, 1, device_id=peer, device_id_type=pl.DeviceIdType.MESH)
-    pl.semaphore_wait(barrier, len(peers))
 
     def remote(source, target, slot, peer):
         return pltpu.make_async_remote_copy(
@@ -177,13 +176,8 @@
             device_id=peer, device_id_type=pl.DeviceIdType.MESH,
         )
 
-    notes = []
-    for k, (source, target) in enumerate(zip(scans + scans, around)):
-        notes.append(remote(source, target, 12 + k, (c, following if k < 2 else prior)))
-        notes[-1].start()
     for load in loads[:4]:
         load.wait()
-    sends = [[], []]
     for d in range(2):
         row, col = corner(here, d, other_cut)
         low, high = near_rows(d, side)
@@ -191,6 +185,13 @@
             near_send[d, plane] = cut_window(
                 ext, plane, row + rim + low, col, high - low, side
             ).astype(jnp.bfloat16)
+    pl.semaphore_wait(barrier, len(peers))
+    notes = []
+    for k, (source, target) in enumerate(zip(scans + scans, around)):
+        notes.append(remote(source, target, 12 + k, (c, following if k < 2 else prior)))
+        notes[-1].start()
+    sends = [[], []]
+    for d in range(2):
         sends[d].append(remote(near_send.at[d], near_in.at[d], 6 * d, (other_cut, region)))
         sends[d][0].start()
         if d == 0:
@@ -264,7 +265,7 @@
             backs.append(
                 remote(far_back.at[d, j], far_out.at[d, j], 6 * d + 4 + j, (q, peer_region))
             )
-        for copy in backs[-3:]:
+        for copy in reversed(backs[-3:]):
             copy.start()
     for copy in sends[0] + sends[1]:
         copy.wait_send()

time: 41.3 us -> 41.6 us (level)
  the two profiles are of different devices: /device:TPU:1 before, /device:TPU:0 now
where the time goes in v5:
time: 41.6 us; the launch traced here: 41.5 us
  Pallas kernels  41.5 us (100%)
    pallas_call x1, Pallas kernels, shards(): pl.pallas_call(functools.partial(wave_kernel, side, count), out_shape=(he...  37.1 us
    pallas_call x1, Pallas kernels, shards(): pl.pallas_call(functools.partial(deposit_kernel, side), out_shape=jax.Sha...  4.33 us

profile of v5, /device:TPU:0, one launch (start us, length us, event | category | flops | bytes accessed | tf_op | source)
XLA Modules:
  0.0 41.5 jit_solution(2660655593530321178)
XLA Ops:
  0.0 37.1 %shard_map.82 = (bf16[2,2,192,256]{3,2,1,0:T(8,128)(2,1)}, bf16[2,2,192,256]{3,2,1,0:T(8,128)(2,1)}, bf16[2,2,2,128,256]{4,3,2,1,0:T(8,128)(2,1)}, s32[4]{0:T(12...) custom-call(s32[4]{0:T(128)} %scans_0_.3, s32[4]{0:T(128)} %scans_1_.3, s32[4]{0:T(128)} %choice_any.1, ...), custom_call_target="tpu_custom_call" | custom-call | tf_op jit(solution)/shard_map/pallas_call | solution.py:332
  37.1 4.3 %shard_map.83 = f32[2,256,1024]{2,1,0:T(8,128)} custom-call(s32[4]{0:T(128)} %scans_0_.3, s32[4]{0:T(128)} %scans_1_.3, s32[4]{0:T(128)} %get-tuple-element.12.around_0_, s32[4]{0:T(128)} %get-tuple-element.13.around_1_, s32[4]{0:T(128)} %get-tuple-element.14.around_2_, s32[4]{0:T(128)} %get-tuple-element.15.around_3_, ...), custom_call_target="tpu_custom_call" | custom-call | tf_op jit(solution)/shard_map/pallas_call | solution.py:355
